TPU v7x, 512 devices: a whole 4x4x16 slice. The times are simulated.
512 devices in a mesh: patch: 512 (over y, x, z, core).
Axes of the slice: x: 4, y: 4, z: 16, core: 2. Of those that a mesh axis runs over, the one named last changes fastest.
Arguments:
- fields: float32 [4, 32, 32, 65536], P(None, None, None, 'patch'), may hold values from -1.5 to 4, as said below
- patch_level: int32 [65536], P('patch'), may hold values from 4 to 6
- relation: int32 [65536, 4], P('patch'), may hold values from 0 to 3
- face_half: int32 [65536, 4], P('patch'), may hold values from 0 to 1
- neighbour: int32 [65536, 4, 2], P('patch'), may hold values from 0 to 255, as said below
- send_list: int32 [512, 16, 8], P('patch'), may hold values from 0 to 127, as said below
Outputs:
- advanced: float32 [4, 32, 32, 65536], P(None, None, None, 'patch')
- time_step: float32 [], replicated
Inputs may be any that keep to these rules, and one draw needn't show every extreme that they name: `send_list`: within each device's block for one curve distance the 8 entries are distinct local patches. `neighbour`: A reference of 128 or more names a slot of a device that exists on the curve. The second reference of a face is used only where relation is 3. `fields`: h lies in [2, 4], |hu| and |hv| at most 1.5, hc in [0, h].
All inputs are finite; a program needn't handle non-finite values.
Results may differ from a plain program's by a relative error of at most 0.0003.
Values sent between devices are 32-bit elements; how exact they have to be, the bound alone decides.
A program may use at most 128 MiB of HBM per device.

v0:
```python
import jax
import jax.numpy as jnp
from jax import lax
from jax.sharding import Mesh
from jax.sharding import PartitionSpec as P

HOPS = 8
NOFF = 16
PATCH = ("patch_0", "patch_1", "patch_2", "patch_3")


courant = 0.4
finest_level = 6.0


def from_behind(array, axis, by):
    devices = lax.axis_size(axis)
    pairs = [(i, i + by) for i in range(devices) if 0 <= i + by < devices]
    return lax.ppermute(array, axis, pairs)


def one_axis_at_a_time(array, axes):
    for axis in axes:
        array = lax.pmin(array, axis)
    return array


def face_strips(state):
    west_side = state[:, 0:4]
    east_side = state[:, ::-1][:, 0:4]
    south_side = jnp.swapaxes(state[:, :, 0:4], 1, 2)
    north_side = jnp.swapaxes(state[:, :, ::-1][:, :, 0:4], 1, 2)
    stacked = jnp.stack([west_side, east_side, south_side, north_side])
    return jnp.transpose(stacked, (4, 0, 1, 2, 3))


def restrict(strip):
    total = strip[..., 0::2, 0::2] + strip[..., 1::2, 0::2]
    total = total + strip[..., 0::2, 1::2]
    total = total + strip[..., 1::2, 1::2]
    return 0.25 * total


def cell_speed(state):
    depth = state[0]
    return jnp.maximum(jnp.abs(state[1] / depth), jnp.abs(state[2] / depth)) + jnp.sqrt(depth)


def fill_ghosts(near, coarse, own_near, relation, face_half):
    cells = near.shape[-1]
    middle = cells // 2
    same_level = near[:, :, 0]
    column = near[:, :, 0, :, 0, :]
    padded = jnp.concatenate([column[..., :1], column, column[..., -1:]], axis=-1)
    slope = padded[..., 2:] - padded[..., :-2]
    upper_half = (face_half == 1)[:, :, None, None]
    base_value = jnp.where(upper_half, column[..., middle:], column[..., :middle])
    base_slope = jnp.where(upper_half, slope[..., middle:], slope[..., :middle])
    base_value = jnp.repeat(base_value, 2, axis=-1)
    base_slope = jnp.repeat(base_slope, 2, axis=-1)
    weights = jnp.where(jnp.arange(cells) % 2 == 1, 0.125, -0.125).astype(near.dtype)
    interpolated = base_value + weights * base_slope
    coarser = jnp.broadcast_to(interpolated[:, :, :, None, :], same_level.shape)
    finer_ghost = jnp.concatenate([coarse[:, :, 0], coarse[:, :, 1]], axis=-1)
    mirror_sign = jnp.array(
        [
            [1.0, -1.0, 1.0, 1.0],
            [1.0, -1.0, 1.0, 1.0],
            [1.0, 1.0, -1.0, 1.0],
            [1.0, 1.0, -1.0, 1.0],
        ],
        near.dtype,
    )
    mirror = own_near * mirror_sign[None, :, :, None, None]
    choose = relation[:, :, None, None, None]
    return jnp.where(
        choose == 0,
        mirror,
        jnp.where(choose == 1, same_level, jnp.where(choose == 2, coarser, finer_ghost)),
    )


def physical(state, normal):
    depth = state[0]
    velocity = state[normal] / depth
    components = [state[normal], state[1] * velocity, state[2] * velocity, state[3] * velocity]
    components[normal] = components[normal] + 0.5 * depth * depth
    return (jnp.stack(components), jnp.abs(velocity) + jnp.sqrt(depth))


def flux_change(padded, normal):
    centre = padded[:, 1:-1]
    slope = 0.5 * (padded[:, 2:] - padded[:, :-2])
    left_state = (centre + 0.5 * slope)[:, :-1]
    right_state = (centre - 0.5 * slope)[:, 1:]
    left_flux, left_speed = physical(left_state, normal)
    right_flux, right_speed = physical(right_state, normal)
    widest = jnp.maximum(left_speed, right_speed)
    numeric_flux = 0.5 * (left_flux + right_flux) - 0.5 * widest * (right_state - left_state)
    return numeric_flux[:, 1:] - numeric_flux[:, :-1]


def advance(state, ghosts, step_ratio):
    sides = jnp.transpose(ghosts, (1, 2, 3, 4, 0))
    along_x = jnp.concatenate([sides[0][:, ::-1], state, sides[1]], axis=1)
    along_y = jnp.concatenate([sides[2][:, ::-1], jnp.swapaxes(state, 1, 2), sides[3]], axis=1)
    change = flux_change(along_x, 1) + jnp.swapaxes(flux_change(along_y, 2), 1, 2)
    return state - step_ratio * change


def hop_blocks(outgoing):
    received = [None] * NOFF
    for towards in (1, -1):
        base_slot = 0 if towards == 1 else HOPS
        blocks = [outgoing[base_slot + distance] for distance in range(HOPS)]
        for section_bit in range(HOPS.bit_length()):
            moving = [distance for distance in range(1, HOPS + 1) if distance >> section_bit & 1]
            stacked = jnp.stack([blocks[distance - 1] for distance in moving])
            arrived = from_behind(stacked, PATCH, towards * (1 << section_bit))
            for position, distance in enumerate(moving):
                blocks[distance - 1] = arrived[position]
        for distance in range(HOPS):
            received[base_slot + distance] = blocks[distance]
    return received


def on_device(fields, patch_level, relation, face_half, neighbour, send_list):
    nfields = fields.shape[0]
    cells = fields.shape[1]
    patches = fields.shape[3]
    spacing = jnp.exp2(finest_level - patch_level.astype(jnp.float32))
    top_speed = jnp.max(cell_speed(fields), axis=(0, 1))
    time_step = courant * one_axis_at_a_time(jnp.min(spacing / top_speed), PATCH)
    step_ratio = time_step / spacing
    strips = face_strips(fields)
    near_part = strips[..., 0:2, :].reshape(patches, 4, nfields, 2 * cells)
    coarse_part = restrict(strips).reshape(patches, 4, nfields, cells)
    own_pack = jnp.concatenate([near_part, coarse_part], axis=-1).reshape(patches, -1)
    outgoing = own_pack[send_list[0]]
    received = hop_blocks(outgoing)
    ghost_pool = jnp.concatenate([own_pack] + received, axis=0)
    opposite = jnp.array([1, 0, 3, 2], jnp.int32)[None, :, None]
    picked = ghost_pool.reshape(ghost_pool.shape[0], 4, -1)[neighbour, opposite]
    whole = picked.reshape(patches, 4, 2, nfields, 3 * cells)
    near = whole[..., : 2 * cells].reshape(patches, 4, 2, nfields, 2, cells)
    coarse = whole[..., 2 * cells :].reshape(patches, 4, 2, nfields, 2, cells // 2)
    ghosts = fill_ghosts(near, coarse, strips[..., 0:2, :], relation, face_half)
    return (advance(fields, ghosts, step_ratio), time_step)


def solution(mesh):
    split = Mesh(mesh.devices.reshape(4, 4, 16, 2), ("patch_0", "patch_1", "patch_2", "patch_3"))
    return jax.shard_map(
        on_device,
        mesh=split,
        in_specs=(
            P(None, None, None, PATCH),
            P(PATCH),
            P(PATCH, None),
            P(PATCH, None),
            P(PATCH, None, None),
            P(PATCH, None, None),
        ),
        out_specs=(P(None, None, None, PATCH), P()),
        check_vma=False,
    )
```

profile of v0, /device:TPU:41, one launch (start us, length us, event | category | flops | bytes accessed | tf_op | source)
XLA Modules:
  0.0 200.5 jit_solution(4860751660609337214)
XLA Ops:
  0.6 3.0 %copy.33 = f32[4,32,32,128]{3,1,2,0:T(8,128)S(1)} copy(f32[4,32,32,128]{3,2,1,0:T(8,128)} %param.8) | data formatting | bytes 4194304 | tf_op args[0]
  3.7 1.3 copy-done.2
  5.2 0.7 slice.337
  5.9 9.6 %slice.338 = f32[128,4,4,2,16]{0,4,3,2,1:T(8,128)} slice(f32[128,4,4,4,32]{0,4,3,2,1:T(8,128)S(1)} %maximum_bitcast_fusion), slice={[0:128:1], [0:4:1], [0:4:1], [1:4:2], [0:32:2]} | slice | bytes 524288 | tf_op jit(solution)/shard_map/slice | solution.py:38
  15.5 9.6 %slice.339 = f32[128,4,4,2,16]{0,4,3,2,1:T(8,128)} slice(f32[128,4,4,4,32]{0,4,3,2,1:T(8,128)S(1)} %maximum_bitcast_fusion), slice={[0:128:1], [0:4:1], [0:4:1], [0:4:2], [1:32:2]} | slice | bytes 524288 | tf_op jit(solution)/shard_map/slice | solution.py:39
  25.1 9.6 %slice.340 = f32[128,4,4,2,16]{0,4,3,2,1:T(8,128)} slice(f32[128,4,4,4,32]{0,4,3,2,1:T(8,128)S(1)} %maximum_bitcast_fusion), slice={[0:128:1], [0:4:1], [0:4:1], [1:4:2], [1:32:2]} | slice | bytes 524288 | tf_op jit(solution)/shard_map/slice | solution.py:40
  34.8 1.2 add_multiply_fusion
  36.0 0.9 pad_maximum_fusion.4
  36.9 1.4 copy.36
  38.5 1.7 gather_fusion
  40.3 1.3 slice_bitcast_fusion.10
  41.5 0.7 pad_maximum_fusion.10
  42.2 2.7 %collective-permute-start.4 = (f32[4,8,1536]{2,1,0:T(8,128)}, f32[4,8,1536]{2,1,0:T(8,128)}, u32[]{:S(2)}, u32[]{:S(2)}) collective-permute-start(f32[4,8,1536]{2,1,0:T(8,128)} %pad_maximum_fusion.10), channel_id=1, source_target_pairs={{1,0},{2,1},{3,2},{4,3},{5,4},{6,5},{7,6},{8,7},{9,8},{10,9},{11,1... | collective-permute-start | bytes 589832 | tf_op jit(solution)/shard_map/ppermute | solution.py:19
  44.9 0.7 pad_maximum_fusion.7
  45.6 3.4 %collective-permute-start = (f32[4,8,1536]{2,1,0:T(8,128)}, f32[4,8,1536]{2,1,0:T(8,128)S(1)}, u32[]{:S(2)}, u32[]{:S(2)}) collective-permute-start(f32[4,8,1536]{2,1,0:T(8,128)} %pad_maximum_fusion.7), channel_id=1, source_target_pairs={{0,1},{1,2},{2,3},{3,4},{4,5},{5,6},{6,7},{7,8},{8,9},{9,10},{10,1... | collective-permute-start | bytes 589832 | tf_op jit(solution)/shard_map/ppermute | solution.py:19
  49.1 8.8 %collective-permute-start.3 = (f32[1,8,1536]{2,1,0:T(8,128)S(1)}, f32[1,8,1536]{2,1,0:T(8,128)}, u32[]{:S(2)}, u32[]{:S(2)}) collective-permute-start(f32[1,8,1536]{2,1,0:T(8,128)S(1)} %get-tuple-element.40), channel_id=1, source_target_pairs={{0,8},{1,9},{2,10},{3,11},{4,12},{5,13},{6,14},{7,15},{8,16},{9,17... | collective-permute-start | bytes 147464 | tf_op jit(solution)/shard_map/ppermute | solution.py:19
  57.9 6.3 %collective-permute-start.7 = (f32[1,8,1536]{2,1,0:T(8,128)S(1)}, f32[1,8,1536]{2,1,0:T(8,128)S(1)}, u32[]{:S(2)}, u32[]{:S(2)}) collective-permute-start(f32[1,8,1536]{2,1,0:T(8,128)S(1)} %get-tuple-element.32), channel_id=1, source_target_pairs={{8,0},{9,1},{10,2},{11,3},{12,4},{13,5},{14,6},{15,7},{16,8},{17,9... | collective-permute-start | bytes 147464 | tf_op jit(solution)/shard_map/ppermute | solution.py:19
  64.2 0.3 add_reduce_fusion
  64.5 1.1 copy.37
  65.6 1.3 divide_reduce_fusion
  66.9 1.2 constant_dynamic-update-slice_fusion
  68.1 7.3 %pmin.28 = f32[]{:T(128)} all-reduce(f32[]{:T(128)} %divide_reduce_fusion), channel_id=1, replica_groups=mesh['patch_0'=4,'patch_1'=4,'patch_2'=16,'patch_3'=2] {'patch_0'}, use_global_device_ids=true, to_apply=%region_2.0 | all-reduce | flops 1 | bytes 8 | tf_op jit(solution)/shard_map/pmin | solution.py:24
  75.5 7.3 %pmin.29 = f32[]{:T(128)} all-reduce(f32[]{:T(128)} %pmin.28), channel_id=1, replica_groups=mesh['patch_0'=4,'patch_1'=4,'patch_2'=16,'patch_3'=2] {'patch_1'}, use_global_device_ids=true, to_apply=%region_3.0 | all-reduce | flops 1 | bytes 8 | tf_op jit(solution)/shard_map/pmin | solution.py:24
  82.8 0.2 copy.54
  83.0 26.9 %pmin.30 = f32[]{:T(128)} all-reduce(f32[]{:T(128)} %pmin.29), channel_id=1, replica_groups=mesh['patch_0'=4,'patch_1'=4,'patch_2'=16,'patch_3'=2] {'patch_2'}, use_global_device_ids=true, to_apply=%region_4.0 | all-reduce | flops 1 | bytes 8 | tf_op jit(solution)/shard_map/pmin | solution.py:24
  109.8 0.2 reshape.152
  110.1 13.9 %pmin.31 = f32[]{:T(128)} all-reduce(f32[]{:T(128)} %pmin.30), channel_id=1, replica_groups=mesh['patch_0'=4,'patch_1'=4,'patch_2'=16,'patch_3'=2] {'patch_3'}, use_global_device_ids=true, to_apply=%region_5.0 | all-reduce | flops 1 | bytes 8 | tf_op jit(solution)/shard_map/pmin | solution.py:24
  124.6 0.7 broadcast_divide_fusion
  125.3 0.9 fusion.30
  126.2 1.9 collective-permute-start.5
  128.2 3.4 %collective-permute-start.1 = (f32[4,8,1536]{2,1,0:T(8,128)S(1)}, f32[4,8,1536]{2,1,0:T(8,128)S(1)}, u32[]{:S(2)}, u32[]{:S(2)}) collective-permute-start(f32[4,8,1536]{2,1,0:T(8,128)S(1)} %pad_maximum_fusion.8), channel_id=1, source_target_pairs={{0,2},{1,3},{2,4},{3,5},{4,6},{5,7},{6,8},{7,9},{8,10},{9,11},{10,... | collective-permute-start | bytes 589832 | tf_op jit(solution)/shard_map/ppermute | solution.py:19
  131.6 2.6 %collective-permute-done.5 = f32[4,8,1536]{2,1,0:T(8,128)S(1)} collective-permute-done((f32[4,8,1536]{2,1,0:T(8,128)S(1)}, f32[4,8,1536]{2,1,0:T(8,128)S(1)}, u32[]{:S(2)}, u32[]{:S(2)}) %collective-permute-start.5) | collective-permute-done | bytes 196640 | tf_op jit(solution)/shard_map/ppermute | solution.py:19
  134.3 11.0 %collective-permute-start.6 = (f32[4,8,1536]{2,1,0:T(8,128)S(1)}, f32[4,8,1536]{2,1,0:T(8,128)S(1)}, u32[]{:S(2)}, u32[]{:S(2)}) collective-permute-start(f32[4,8,1536]{2,1,0:T(8,128)S(1)} %pad_maximum_fusion.12), channel_id=1, source_target_pairs={{4,0},{5,1},{6,2},{7,3},{8,4},{9,5},{10,6},{11,7},{12,8},{13,9},{1... | collective-permute-start | bytes 589832 | tf_op jit(solution)/shard_map/ppermute | solution.py:19
  145.3 2.1 %collective-permute-start.2 = (f32[4,8,1536]{2,1,0:T(8,128)S(1)}, f32[4,8,1536]{2,1,0:T(8,128)S(1)}, u32[]{:S(2)}, u32[]{:S(2)}) collective-permute-start(f32[4,8,1536]{2,1,0:T(8,128)S(1)} %pad_maximum_fusion.9), channel_id=1, source_target_pairs={{0,4},{1,5},{2,6},{3,7},{4,8},{5,9},{6,10},{7,11},{8,12},{9,13},{1... | collective-permute-start | bytes 589832 | tf_op jit(solution)/shard_map/ppermute | solution.py:19
  147.5 15.7 %collective-permute-done.2 = f32[4,8,1536]{2,1,0:T(8,128)S(1)} collective-permute-done((f32[4,8,1536]{2,1,0:T(8,128)S(1)}, f32[4,8,1536]{2,1,0:T(8,128)S(1)}, u32[]{:S(2)}, u32[]{:S(2)}) %collective-permute-start.2) | collective-permute-done | bytes 196640 | tf_op jit(solution)/shard_map/ppermute | solution.py:19
  163.3 0.8 copy_dynamic-update-slice_fusion.8
  164.4 10.4 %gather_fusion.1 = f32[1024,384]{1,0:T(8,128)} fusion(f32[256,4,384]{2,1,0:T(4,128)S(1)} %copy_dynamic-update-slice_fusion, s32[1024]{0:T(1024)S(1)} %reshape.152), kind=kCustom, calls=%fused_computation.1 | custom fusion | bytes 3153920 | tf_op jit(solution)/shard_map/gather | solution.py:143
  174.8 2.5 %reshape.139 = f32[128,4,2,4,96]{4,3,2,1,0:T(4,128)S(1)} reshape(f32[1024,384]{1,0:T(8,128)} %gather_fusion.1) | data formatting | bytes 3145728 | tf_op jit(solution)/shard_map/reshape | solution.py:144
  177.3 2.5 %slice.493 = f32[128,4,2,4,32]{4,3,2,1,0:T(4,128)} slice(f32[128,4,2,4,96]{4,3,2,1,0:T(4,128)S(1)} %reshape.139), slice={[0:128], [0:4], [0:2], [0:4], [64:96]} | slice | bytes 1048576 | tf_op jit(solution)/shard_map/slice | solution.py:146
  179.8 1.7 copy.55
  181.5 1.2 copy.72
  182.7 1.0 slice_bitcast_fusion.3
  183.7 2.0 copy.73
  185.9 0.1 broadcast_in_dim.72
  186.0 0.1 broadcast_in_dim.75
  186.3 0.7 copy-done.5
  186.9 0.1 fusion.22
  187.1 0.1 copy.60
  187.2 0.1 copy.62
  187.3 0.4 copy-done.3
  187.7 0.9 fusion.13
  188.6 0.6 multiply_bitcast_fusion.1
  189.2 0.6 fusion.16
  189.7 0.8 fusion.3
  190.6 1.7 slice_subtract_fusion.3
  192.3 0.1 copy.67
  192.4 0.1 copy.68
  192.5 0.3 copy-done.1
  192.8 0.9 fusion.15
  193.6 0.6 multiply_bitcast_fusion
  194.2 0.5 slice_multiply_fusion.1
  194.8 0.7 fusion.1
  195.5 0.9 copy-done.6
  196.3 3.0 %fusion.11 = f32[4,32,32,128]{3,2,1,0:T(8,128)} fusion(f32[4,32,32,128]{3,2,1,0:T(8,128)S(1)} %copy-done.1, f32[4,33,32,128]{3,1,2,0:T(8,128)S(1)} %fusion.1, f32[4,32,32,128]{3,1,2,0:T(8,128)S(1)} %copy-done.6, f32[128]{0:T(128)S(1)} %broadcast_divide_fusion), kind=kLoop, calls=%fused_computation.24 | loop fusion | flops 2097152 | bytes 10486272 | tf_op jit(solution)/shard_map/sub | solution.py:108
  (77 shorter events, 1.4 us)
Async XLA Ops:
  0.6 3.0 %copy-start = (f32[4,32,32,128]{3,2,1,0:T(8,128)S(1)}, f32[4,32,32,128]{3,2,1,0:T(8,128)}, u32[]{:S(2)}) copy-start(f32[4,32,32,128]{3,2,1,0:T(8,128)} %param.8) | copy-start | bytes 6291460
  3.6 1.3 copy-start.2
  5.1 31.8 %copy-start.4 = (f32[128,4,4,4,32]{0,4,3,2,1:T(8,128)}, f32[128,4,4,4,32]{0,4,3,2,1:T(8,128)S(1)}, u32[]{:S(2)}) copy-start(f32[128,4,4,4,32]{0,4,3,2,1:T(8,128)S(1)} %maximum_bitcast_fusion) | copy-start | bytes 3145732
  34.7 3.6 %copy-start.8 = (s32[1,16,8]{1,2,0:T(8,128)S(1)}, s32[1,16,8]{1,2,0:T(8,128)}, u32[]{:S(2)}) copy-start(s32[1,16,8]{1,2,0:T(8,128)} %param.13) | copy-start | bytes 1540
  40.3 24.2 %copy-start.7 = (f32[128,4,4,96]{0,3,2,1:T(8,128)S(1)}, f32[128,4,4,96]{0,3,2,1:T(8,128)}, u32[]{:S(2)}) copy-start(f32[128,4,4,96]{0,3,2,1:T(8,128)} %pad_maximum_fusion.4) | copy-start | bytes 2359300
  40.3 25.3 %copy-start.10 = (s32[128,4]{0,1:T(4,128)S(1)}, s32[128,4]{0,1:T(4,128)}, u32[]{:S(2)}) copy-start(s32[128,4]{0,1:T(4,128)} %param.11) | copy-start | bytes 6148
  40.3 25.4 %copy-start.11 = (s32[128,4]{0,1:T(4,128)S(1)}, s32[128,4]{0,1:T(4,128)}, u32[]{:S(2)}) copy-start(s32[128,4]{0,1:T(4,128)} %param.10) | copy-start | bytes 6148
  42.2 40.5 %copy-start.9 = (s32[128,4,2]{0,2,1:T(2,128)S(1)}, s32[128,4,2]{0,2,1:T(2,128)}, u32[]{:S(2)}) copy-start(s32[128,4,2]{0,2,1:T(2,128)} %param.12) | copy-start | bytes 12292
  42.2 40.5 %copy-start.13 = (s32[4]{0:T(128)S(1)}, s32[4]{0:T(128)}, u32[]{:S(2)}) copy-start(s32[4]{0:T(128)} %constant.81) | copy-start | bytes 52
  42.2 83.1 %collective-permute-start.4 = (f32[4,8,1536]{2,1,0:T(8,128)}, f32[4,8,1536]{2,1,0:T(8,128)}, u32[]{:S(2)}, u32[]{:S(2)}) collective-permute-start(f32[4,8,1536]{2,1,0:T(8,128)} %pad_maximum_fusion.10), channel_id=1, source_target_pairs={{1,0},{2,1},{3,2},{4,3},{5,4},{6,5},{7,6},{8,7},{9,8},{10,9},{11,1... | collective-permute-start | bytes 589832 | tf_op jit(solution)/shard_map/ppermute | solution.py:19
  45.6 82.5 %collective-permute-start = (f32[4,8,1536]{2,1,0:T(8,128)}, f32[4,8,1536]{2,1,0:T(8,128)S(1)}, u32[]{:S(2)}, u32[]{:S(2)}) collective-permute-start(f32[4,8,1536]{2,1,0:T(8,128)} %pad_maximum_fusion.7), channel_id=1, source_target_pairs={{0,1},{1,2},{2,3},{3,4},{4,5},{5,6},{6,7},{7,8},{8,9},{9,10},{10,1... | collective-permute-start | bytes 589832 | tf_op jit(solution)/shard_map/ppermute | solution.py:19
  49.1 114.2 %collective-permute-start.3 = (f32[1,8,1536]{2,1,0:T(8,128)S(1)}, f32[1,8,1536]{2,1,0:T(8,128)}, u32[]{:S(2)}, u32[]{:S(2)}) collective-permute-start(f32[1,8,1536]{2,1,0:T(8,128)S(1)} %get-tuple-element.40), channel_id=1, source_target_pairs={{0,8},{1,9},{2,10},{3,11},{4,12},{5,13},{6,14},{7,15},{8,16},{9,17... | collective-permute-start | bytes 147464 | tf_op jit(solution)/shard_map/ppermute | solution.py:19
  57.9 106.5 %collective-permute-start.7 = (f32[1,8,1536]{2,1,0:T(8,128)S(1)}, f32[1,8,1536]{2,1,0:T(8,128)S(1)}, u32[]{:S(2)}, u32[]{:S(2)}) collective-permute-start(f32[1,8,1536]{2,1,0:T(8,128)S(1)} %get-tuple-element.32), channel_id=1, source_target_pairs={{8,0},{9,1},{10,2},{11,3},{12,4},{13,5},{14,6},{15,7},{16,8},{17,9... | collective-permute-start | bytes 147464 | tf_op jit(solution)/shard_map/ppermute | solution.py:19
  126.2 8.0 %collective-permute-start.5 = (f32[4,8,1536]{2,1,0:T(8,128)S(1)}, f32[4,8,1536]{2,1,0:T(8,128)S(1)}, u32[]{:S(2)}, u32[]{:S(2)}) collective-permute-start(f32[4,8,1536]{2,1,0:T(8,128)S(1)} %pad_maximum_fusion.11), channel_id=1, source_target_pairs={{2,0},{3,1},{4,2},{5,3},{6,4},{7,5},{8,6},{9,7},{10,8},{11,9},{12,... | collective-permute-start | bytes 589832 | tf_op jit(solution)/shard_map/ppermute | solution.py:19
  128.2 17.1 %collective-permute-start.1 = (f32[4,8,1536]{2,1,0:T(8,128)S(1)}, f32[4,8,1536]{2,1,0:T(8,128)S(1)}, u32[]{:S(2)}, u32[]{:S(2)}) collective-permute-start(f32[4,8,1536]{2,1,0:T(8,128)S(1)} %pad_maximum_fusion.8), channel_id=1, source_target_pairs={{0,2},{1,3},{2,4},{3,5},{4,6},{5,7},{6,8},{7,9},{8,10},{9,11},{10,... | collective-permute-start | bytes 589832 | tf_op jit(solution)/shard_map/ppermute | solution.py:19
  134.3 29.9 %collective-permute-start.6 = (f32[4,8,1536]{2,1,0:T(8,128)S(1)}, f32[4,8,1536]{2,1,0:T(8,128)S(1)}, u32[]{:S(2)}, u32[]{:S(2)}) collective-permute-start(f32[4,8,1536]{2,1,0:T(8,128)S(1)} %pad_maximum_fusion.12), channel_id=1, source_target_pairs={{4,0},{5,1},{6,2},{7,3},{8,4},{9,5},{10,6},{11,7},{12,8},{13,9},{1... | collective-permute-start | bytes 589832 | tf_op jit(solution)/shard_map/ppermute | solution.py:19
  145.3 17.9 %collective-permute-start.2 = (f32[4,8,1536]{2,1,0:T(8,128)S(1)}, f32[4,8,1536]{2,1,0:T(8,128)S(1)}, u32[]{:S(2)}, u32[]{:S(2)}) collective-permute-start(f32[4,8,1536]{2,1,0:T(8,128)S(1)} %pad_maximum_fusion.9), channel_id=1, source_target_pairs={{0,4},{1,5},{2,6},{3,7},{4,8},{5,9},{6,10},{7,11},{8,12},{9,13},{1... | collective-permute-start | bytes 589832 | tf_op jit(solution)/shard_map/ppermute | solution.py:19
  185.7 1.2 copy-start.5
  185.7 1.2 copy-start.12
  186.0 1.7 copy-start.3
  190.6 2.2 %copy-start.1 = (f32[4,32,32,128]{3,2,1,0:T(8,128)S(1)}, f32[4,32,32,128]{3,2,1,0:T(8,128)}, u32[]{:S(2)}) copy-start(f32[4,32,32,128]{3,2,1,0:T(8,128)} %param.8) | copy-start | bytes 6291460
  194.8 1.6 copy-start.6
where the time goes:
time: 201 us; the launch traced here: 200 us
  local copies, waits for them, and re-layouts  67.6 us (34%)
  blocking collectives  55.3 us (28%)
  starting transfers between devices  39.6 us (20%)
  waiting for transfers between devices  18.3 us (9%)
  other arithmetic  16.6 us (8%)
  between operations  3.03 us (2%)
    pmin x4, blocking collectives, one_axis_at_a_time(): array = lax.pmin(array, axis)  55.3 us
    ppermute x8, starting transfers between devices, from_behind(): return lax.ppermute(array, axis, pairs)  39.6 us
    ppermute x8, waiting for transfers between devices, from_behind(): return lax.ppermute(array, axis, pairs)  18.3 us
    gather x1, local copies, waits for them, and re-layouts, on_device(): picked = ghost_pool.reshape(ghost_pool.shape[0], 4, -1)[neighbour, opposite]  10.4 us
    slice x2, local copies, waits for them, and re-layouts, restrict(): total = strip[..., 0::2, 0::2] + strip[..., 1::2, 0::2]  10.4 us
    slice x1, local copies, waits for them, and re-layouts, restrict(): total = total + strip[..., 1::2, 1::2]  9.65 us
    slice x1, local copies, waits for them, and re-layouts, restrict(): total = total + strip[..., 0::2, 1::2]  9.56 us
    unnamed x45, local copies, waits for them, and re-layouts  8.78 us
  transfers between devices with their start and end apart: 8, of which 2 were waited for; matrix products, arithmetic and copies ran while one was open for 4% of the time, Pallas kernels for 0%

commit v1 on v0

v1 whole, which is shorter than its diff:
```python
import jax
import jax.numpy as jnp
from jax import lax
from jax.experimental import pallas as pl
from jax.experimental.pallas import tpu as pltpu
from jax.sharding import PartitionSpec as P

MESH = pl.DeviceIdType.MESH
CELLS = 32
NF = 4
LANES = 128
HOPS = 8
SEND = 8
PLANES = CELLS + 4
ROWS = 80
HALF = 8 * ROWS
DIM_Y, DIM_X, DIM_Z = 4, 4, 16
NEAR_Z = 4
COURANT = 0.4
F32 = jnp.float32


def offsets():
    return [k + 1 for k in range(HOPS)] + [-(k + 1) for k in range(HOPS)]


def wave(depth):
    r = lax.rsqrt(depth)
    return r * r, depth * r


def physical(state, normal):
    inverse, root = wave(state[0])
    momentum = state[normal]
    velocity = momentum * inverse
    flux = [momentum, state[1] * velocity, state[2] * velocity, state[3] * velocity]
    flux[normal] = flux[normal] + 0.5 * (state[0] * state[0])
    return flux, jnp.abs(velocity) + root


def cell_sides(load, j):
    uppers, lowers = [], []
    for c in range(NF):
        here = load(c, j)
        delta = 0.25 * (load(c, j + 1) - load(c, j - 1))
        uppers.append(here + delta)
        lowers.append(here - delta)
    return uppers, lowers


def interface(left, left_flux, left_speed, right, right_flux, right_speed):
    widest = jnp.maximum(left_speed, right_speed)
    return [(left_flux[c] + right_flux[c]) - widest * (right[c] - left[c]) for c in range(NF)]


def body(fields, level, relation, half, near, sends, out, step_out,
         px, py, cx, cy, level_v, relation_v, half_v, near_v, sends_v,
         own, own0, far, far0, send0, send1, recv0, recv1, edge, coarse, low,
         low_x, low_y, low_c, low_a, low_b, got_a,
         load_sem, small_sem, bulk_send, bulk_recv, low_send, low_recv):
    me = lax.axis_index("patch")
    core = lax.rem(me, 2)
    z = lax.rem(me // 2, DIM_Z)
    x = lax.rem(me // (2 * DIM_Z), DIM_X)
    y = me // (2 * DIM_Z * DIM_X)
    total = DIM_Y * DIM_X * DIM_Z * 2

    def place(yy, xx, zz, cc):
        return ((yy * DIM_X + xx) * DIM_Z + zz) * 2 + cc

    curve = [lax.rem(me + o + total, total) for o in offsets()]
    along_x = [place(y, lax.rem(x + k, DIM_X), z, core) for k in range(1, DIM_X)]
    along_y = [place(lax.rem(y + k, DIM_Y), x, z, core) for k in range(1, DIM_Y)]
    other = [place(y, x, z, 1 - core)]
    steps_z = [k for k in range(-NEAR_Z, NEAR_Z + 1) if k]
    along_z = [place(y, x, lax.rem(z + k + DIM_Z, DIM_Z), core) for k in steps_z]
    ends_z = [along_z[0], along_z[-1]]

    barrier = pltpu.get_barrier_semaphore()
    partners = curve + along_x + along_y + other + along_z
    for partner in partners:
        pl.semaphore_signal(barrier, inc=1, device_id=(partner,), device_id_type=MESH)

    loads = [pltpu.make_async_copy(fields.at[c], px.at[c, pl.ds(2, CELLS)], load_sem.at[c]) for c in range(NF)]
    smalls = [
        pltpu.make_async_copy(source, target, small_sem.at[n])
        for n, (source, target) in enumerate(
            [(level, level_v), (relation, relation_v), (half, half_v), (near, near_v), (sends, sends_v)]
        )
    ]
    for copy in loads + smalls:
        copy.start()
    for copy in loads + smalls:
        copy.wait()

    px2 = px.reshape(NF * PLANES * CELLS, LANES)
    py2 = py.reshape(NF * PLANES * CELLS, LANES)
    cy2 = cy.reshape(NF * CELLS * CELLS, LANES)
    out2 = out.reshape(NF * CELLS * CELLS, LANES)

    def scan_plane(i, best):
        state = [px[c, i + 2] for c in range(NF)]
        for c in range(NF):
            py2[pl.ds((c * PLANES + 2) * CELLS + i, CELLS, stride=CELLS), :] = state[c]
        inverse, root = wave(state[0])
        return jnp.maximum(best, jnp.maximum(jnp.abs(state[1]), jnp.abs(state[2])) * inverse + root)

    best = lax.fori_loop(0, CELLS, scan_plane, jnp.zeros((CELLS, LANES), F32), unroll=4)
    top_speed = jnp.max(best, axis=0, keepdims=True)
    spacing = lax.shift_left(jnp.ones((1, LANES), jnp.int32), 6 - level_v[...]).astype(F32)
    low[...] = spacing / top_speed

    def restricted(ref, first, second):
        evens = ref[pl.ds(first, 16, stride=2), :] + ref[pl.ds(second, 16, stride=2), :]
        odds = ref[pl.ds(first + 1, 16, stride=2), :] + ref[pl.ds(second + 1, 16, stride=2), :]
        return 0.25 * (evens + odds)

    for face in range(4):
        planes = px2 if face < 2 else py2
        for c in range(NF):
            at = [(c * PLANES + (2 + k if face % 2 == 0 else 33 - k)) * CELLS for k in range(4)]
            row = (face * NF + c) * ROWS
            own[pl.ds(row, CELLS), :] = planes[pl.ds(at[0], CELLS), :]
            own[pl.ds(row + 32, CELLS), :] = planes[pl.ds(at[1], CELLS), :]
            own[pl.ds(row + 64, 16), :] = restricted(planes, at[2], at[3])
            own0[pl.ds((face * NF + c) * 16, 16), :] = restricted(planes, at[0], at[1])

    lane = lax.broadcasted_iota(jnp.int32, (SEND, LANES), 1)
    slot = lax.broadcasted_iota(jnp.int32, (SEND, LANES), 0)
    listed = jnp.take_along_axis(sends_v[...], lane // SEND, axis=1)
    listed = jnp.sum(jnp.where(lax.rem(lane, SEND) == slot, listed, 0), axis=0, keepdims=True)
    listed = jnp.broadcast_to(listed, (LANES, LANES))
    for block in range(10):
        picked = jnp.take_along_axis(own[pl.ds(block * LANES, LANES), :], listed, axis=1)
        target = send0 if block < 5 else send1
        target[:, pl.ds(block % 5 * LANES, LANES)] = picked.T

    pl.semaphore_wait(barrier, len(partners))

    def tell(value, targets, slots, stage):
        for n, target in enumerate(targets):
            pltpu.make_async_remote_copy(
                src_ref=value, dst_ref=slots.at[n], send_sem=low_send.at[stage], recv_sem=low_recv.at[stage],
                device_id=(target,), device_id_type=MESH,
            ).start()

    def hear(slots, stage):
        pltpu.make_async_copy(slots, slots, low_recv.at[stage]).wait()
        return jnp.min(slots[...], axis=0)

    def exchange(source, target, part, which):
        for k in which:
            rows = pl.ds(k * SEND, SEND)
            pltpu.make_async_remote_copy(
                src_ref=source.at[rows], dst_ref=target.at[rows], send_sem=bulk_send.at[part],
                recv_sem=bulk_recv.at[part], device_id=(curve[k],), device_id_type=MESH,
            ).start()

    far_first = [7, 15, 6, 14, 5, 13, 4, 12, 3, 11, 2, 10, 1, 9, 0, 8]
    tell(low, along_z, low_a, 0)
    exchange(send0, recv0, 0, far_first)

    def interior(ref, normal, change):
        def row_tile(t, carry):
            rows = pl.ds(pl.multiple_of(t * 8, 8), 8)

            def load(c, j):
                return ref[c, j, rows, :]

            def advance(j, carried):
                left, left_flux, left_speed, before = carried
                upper, right = cell_sides(load, j + 1)
                right_flux, right_speed = physical(right, normal)
                flux = interface(left, left_flux, left_speed, right, right_flux, right_speed)
                for c in range(NF):
                    change[c, j - 2, rows, :] = flux[c] - before[c]
                upper_flux, upper_speed = physical(upper, normal)
                return upper, upper_flux, upper_speed, flux

            first, _ = cell_sides(load, 3)
            first_flux, first_speed = physical(first, normal)
            zero = jnp.zeros((8, LANES), F32)
            carried = advance(3, (first, first_flux, first_speed, [zero] * NF))
            last = lax.fori_loop(4, 32, advance, carried, unroll=4)
            for c in range(NF):
                change[c, 0, rows, :] = zero
                change[c, 30, rows, :] = -last[3][c]
                change[c, 31, rows, :] = zero
            return carry

        lax.fori_loop(0, 4, row_tile, 0)

    interior(px, 1, cx)

    lowest = jnp.minimum(low[...], hear(low_a, 0))
    got_a[...] = lowest
    tell(got_a, ends_z, low_b, 1)
    exchange(send1, recv1, 1, far_first)

    interior(py, 2, cy)

    lowest = jnp.minimum(lowest, hear(low_b, 1))
    low_x[0] = lowest
    tell(low_x.at[0], along_x, low_x.at[pl.ds(1, 3)], 2)
    lowest = jnp.minimum(lowest, hear(low_x.at[pl.ds(1, 3)], 2))
    low_y[0] = lowest
    tell(low_y.at[0], along_y, low_y.at[pl.ds(1, 3)], 3)
    lowest = jnp.minimum(lowest, hear(low_y.at[pl.ds(1, 3)], 3))
    low_c[0] = lowest
    tell(low_c.at[0], other, low_c.at[pl.ds(1, 1)], 4)
    lowest = jnp.minimum(lowest, hear(low_c.at[pl.ds(1, 1)], 4))
    time_step = COURANT * jnp.min(lowest, axis=1, keepdims=True)
    step_out[...] = jnp.broadcast_to(time_step, (1, LANES))
    ratio = jnp.broadcast_to(0.5 * (time_step / spacing), (CELLS, LANES))

    def settle(i, carry):
        for c in range(NF):
            turned = cy2[pl.ds(c * CELLS * CELLS + i, CELLS, stride=CELLS), :]
            out[c, i] = px[c, i + 2] - ratio * (cx[c, i] + turned)
        return carry

    lax.fori_loop(0, CELLS, settle, 0, unroll=2)

    def unpack(part):
        target = recv0 if part == 0 else recv1
        pltpu.make_async_copy(target, target, bulk_recv.at[part]).wait()
        for block in range(5):
            far[pl.ds((part * 5 + block) * LANES, LANES), :] = target[:, pl.ds(block * LANES, LANES)].T
        for face in (2 * part, 2 * part + 1):
            for c in range(NF):
                row = (face * NF + c) * ROWS
                far0[pl.ds((face * NF + c) * 16, 16), :] = restricted(far, row, row + 32)

    def pick(mine, theirs, row, count, index):
        spot = jnp.broadcast_to(lax.rem(index, LANES), (count, LANES))
        remote = jnp.broadcast_to(index, (count, LANES)) >= LANES
        return jnp.where(
            remote,
            jnp.take_along_axis(theirs[pl.ds(row, count), :], spot, axis=1),
            jnp.take_along_axis(mine[pl.ds(row, count), :], spot, axis=1),
        )

    def ghosts(face):
        planes = px if face < 2 else py
        opposite = face ^ 1
        kind = jnp.broadcast_to(relation_v[pl.ds(face, 1), :], (CELLS, LANES))
        upper = jnp.broadcast_to(half_v[pl.ds(face, 1), :], (16, LANES)) == 1
        first = near_v[face, pl.ds(0, 1), :]
        second = near_v[face, pl.ds(1, 1), :]
        for c in range(NF):
            row = (opposite * NF + c) * ROWS
            row0 = (opposite * NF + c) * 16
            level_same = [pick(own, far, row + 32 * g, CELLS, first) for g in range(2)]
            finer = [
                jnp.concatenate([pick(own0, far0, row0, 16, first), pick(own0, far0, row0, 16, second)], axis=0),
                jnp.concatenate([pick(own, far, row + 64, 16, first), pick(own, far, row + 64, 16, second)], axis=0),
            ]
            value = level_same[0]
            edge[pl.ds(8, CELLS), :] = value
            edge[pl.ds(7, 1), :] = value[0:1]
            edge[pl.ds(40, 1), :] = value[31:32]
            slope = edge[pl.ds(9, CELLS), :] - edge[pl.ds(7, CELLS), :]
            base = jnp.where(upper, value[16:], value[:16])
            lean = 0.125 * jnp.where(upper, slope[16:], slope[:16])
            coarse[pl.ds(0, 16, stride=2), :] = base - lean
            coarse[pl.ds(1, 16, stride=2), :] = base + lean
            wide = coarse[...]
            sign = -1.0 if c == 1 + face // 2 else 1.0
            for g in range(2):
                mirror = sign * own[pl.ds((face * NF + c) * ROWS + 32 * g, CELLS), :]
                ghost = jnp.where(
                    kind == 0,
                    mirror,
                    jnp.where(kind == 1, level_same[g], jnp.where(kind == 2, wide, finer[g])),
                )
                planes[c, 1 - g if face % 2 == 0 else 34 + g] = ghost

    def rim(ref, normal, apply):
        def load(c, j):
            return ref[c, j]

        for start, cells in ((1, ((0, -1, 0), (1, 1, None))), (32, ((30, None, 0), (31, 0, 1)))):
            sides = [cell_sides(load, j) for j in (start, start + 1, start + 2)]
            flux = []
            for n in range(2):
                left, right = sides[n][0], sides[n + 1][1]
                left_flux, left_speed = physical(left, normal)
                right_flux, right_speed = physical(right, normal)
                flux.append(interface(left, left_flux, left_speed, right, right_flux, right_speed))
            for c in range(NF):
                if start == 1:
                    apply(c, 0, flux[1][c] - flux[0][c])
                    apply(c, 1, -flux[1][c])
                else:
                    apply(c, 30, flux[0][c])
                    apply(c, 31, flux[1][c] - flux[0][c])

    def apply_x(c, i, change):
        out[c, i] = out[c, i] - ratio * change

    def apply_y(c, j, change):
        rows = pl.ds(c * CELLS * CELLS + j, CELLS, stride=CELLS)
        out2[rows, :] = out2[rows, :] - ratio * change

    unpack(0)
    ghosts(0)
    ghosts(1)
    rim(px, 1, apply_x)
    unpack(1)
    ghosts(2)
    ghosts(3)
    rim(py, 2, apply_y)

    for part, source in enumerate((send0, send1)):
        pltpu.make_async_copy(source, source, bulk_send.at[part]).wait()
    for stage, slots in enumerate((low_a, low_b, low_x.at[pl.ds(1, 3)], low_y.at[pl.ds(1, 3)], low_c.at[pl.ds(1, 1)])):
        pltpu.make_async_copy(slots, slots, low_send.at[stage]).wait()


def on_device(fields, patch_level, relation, face_half, neighbour, send_list):
    any_space = pl.BlockSpec(memory_space=pl.ANY)
    vmem = pl.BlockSpec(memory_space=pltpu.VMEM)
    cube = (NF, CELLS, CELLS, LANES)
    advanced, step = pl.pallas_call(
        body,
        out_shape=(jax.ShapeDtypeStruct(cube, F32), jax.ShapeDtypeStruct((1, LANES), F32)),
        in_specs=[any_space] * 6,
        out_specs=(vmem, vmem),
        scratch_shapes=[
            pltpu.VMEM((NF, PLANES, CELLS, LANES), F32),
            pltpu.VMEM((NF, PLANES, CELLS, LANES), F32),
            pltpu.VMEM(cube, F32),
            pltpu.VMEM(cube, F32),
            pltpu.VMEM((1, LANES), jnp.int32),
            pltpu.VMEM((4, LANES), jnp.int32),
            pltpu.VMEM((4, LANES), jnp.int32),
            pltpu.VMEM((4, 2, LANES), jnp.int32),
            pltpu.VMEM((SEND, LANES), jnp.int32),
            pltpu.VMEM((16 * ROWS, LANES), F32),
            pltpu.VMEM((256, LANES), F32),
            pltpu.VMEM((16 * ROWS, LANES), F32),
            pltpu.VMEM((256, LANES), F32),
            pltpu.VMEM((LANES, HALF), F32),
            pltpu.VMEM((LANES, HALF), F32),
            pltpu.VMEM((LANES, HALF), F32),
            pltpu.VMEM((LANES, HALF), F32),
            pltpu.VMEM((48, LANES), F32),
            pltpu.VMEM((CELLS, LANES), F32),
            pltpu.VMEM((1, LANES), F32),
            pltpu.VMEM((DIM_X, 1, LANES), F32),
            pltpu.VMEM((DIM_Y, 1, LANES), F32),
            pltpu.VMEM((2, 1, LANES), F32),
            pltpu.VMEM((2 * NEAR_Z, 1, LANES), F32),
            pltpu.VMEM((2, 1, LANES), F32),
            pltpu.VMEM((1, LANES), F32),
            pltpu.SemaphoreType.DMA((NF,)),
            pltpu.SemaphoreType.DMA((5,)),
            pltpu.SemaphoreType.DMA((2,)),
            pltpu.SemaphoreType.DMA((2,)),
            pltpu.SemaphoreType.DMA((5,)),
            pltpu.SemaphoreType.DMA((5,)),
        ],
        compiler_params=pltpu.CompilerParams(collective_id=0, has_side_effects=True),
    )(
        fields,
        patch_level.reshape(1, LANES),
        relation.T,
        face_half.T,
        jnp.transpose(neighbour, (1, 2, 0)),
        jnp.pad(send_list[0].T, ((0, 0), (0, LANES - NSLOT))),
    )
    return advanced, step[0, 0]


NSLOT = 2 * HOPS


def solution(mesh):
    return jax.shard_map(
        on_device,
        mesh=mesh,
        in_specs=(
            P(None, None, None, "patch"),
            P("patch"),
            P("patch", None),
            P("patch", None),
            P("patch", None, None),
            P("patch", None, None),
        ),
        out_specs=(P(None, None, None, "patch"), P()),
        check_vma=False,
    )
```

time: 201 us -> 50.1 us (0.25)
  the two profiles are of different devices: /device:TPU:41 before, /device:TPU:1 now
where the time goes in v1:
time: 50.1 us; the launch traced here: 49.9 us
  Pallas kernels  43.7 us (87%)
  local copies, waits for them, and re-layouts  4.37 us (9%)
  between operations  1.81 us (4%)
    pallas_call x1, Pallas kernels, on_device(): pl.pallas_call(body, out_shape=(jax.ShapeDtypeStruct(cube, F32), jax.Shap...  43.7 us
    unnamed x3, local copies, waits for them, and re-layouts  3.08 us
    pad x1, local copies, waits for them, and re-layouts, on_device(): jnp.pad(send_list[0].T, ((0, 0), (0, LANES - NSLOT)))  1.28 us

profile of v1, /device:TPU:1, one launch (start us, length us, event | category | flops | bytes accessed | tf_op | source)
XLA Modules:
  0.0 49.9 jit_solution(9386645805127955757)
XLA Ops:
  0.6 1.3 %pad.4.sends = s32[8,128]{1,0:T(8,128)} pad(s32[8,16]{1,0:T(8,128)} %bitcast.10, s32[]{:T(128)} %constant.0.clone.1), padding=0_0x0_112 | pad | bytes 4612 | tf_op jit(solution)/shard_map/jit(_pad)/pad | solution.py:370
  1.9 43.7 %shard_map.77 = (f32[4,32,32,128]{3,2,1,0:T(8,128)}, f32[1,128]{1,0:T(1,128)}) custom-call(f32[4,32,32,128]{3,2,1,0:T(8,128)} %fields.1, s32[1,128]{1,0:T(1,128)} %bitcast.13, s32[4,128]{1,0:T(4,128)} %bitcast.11, s32[4,128]{1,0:T(4,128)} %bitcast.12, s32[4,2,128]{2,1,0:T(2,128)} %bitcast.9, s32[8,128]{1,0:T(8,128)} %pad.4.sends), custom_call_target="tpu_custom_call" | custom-call | tf_op jit(solution)/shard_map/pallas_call | solution.py:324
  45.7 0.0 copy-start
  45.7 3.1 %copy.10 = f32[4,32,32,128]{3,2,1,0:T(8,128)} copy(f32[4,32,32,128]{3,2,1,0:T(8,128)} %get-tuple-element.8) | data formatting | bytes 4194304
  48.7 0.0 copy-done
Async XLA Ops:
  45.7 3.1 %copy-start = (f32[1,128]{1,0:T(1,128)S(1)}, f32[1,128]{1,0:T(1,128)}, u32[]{:S(2)}) copy-start(f32[1,128]{1,0:T(1,128)} %get-tuple-element.5) | copy-start | bytes 1540

commit v2 on v1

v2 whole, which is shorter than its diff:
```python
import jax
import jax.numpy as jnp
from jax import lax
from jax.experimental import pallas as pl
from jax.experimental.pallas import tpu as pltpu
from jax.sharding import PartitionSpec as P

MESH = pl.DeviceIdType.MESH
CELLS = 32
NF = 4
LANES = 128
HOPS = 8
SEND = 8
PLANES = CELLS + 4
ROWS = 80
NSLOT = 2 * HOPS
PARTS = ((0, 3), (3, 2), (5, 3), (8, 2))
FAR_FIRST = [7, 15, 6, 14, 5, 13, 4, 12, 3, 11, 2, 10, 1, 9, 0, 8]
DIM_Y, DIM_X, DIM_Z = 4, 4, 16
NEAR_Z = 4
COURANT = 0.4
F32 = jnp.float32


def offsets():
    return [k + 1 for k in range(HOPS)] + [-(k + 1) for k in range(HOPS)]


def wave(depth):
    r = lax.rsqrt(depth)
    return r * r, depth * r


def physical(state, normal):
    inverse, root = wave(state[0])
    momentum = state[normal]
    velocity = momentum * inverse
    flux = [momentum, state[1] * velocity, state[2] * velocity, state[3] * velocity]
    flux[normal] = flux[normal] + 0.5 * (state[0] * state[0])
    return flux, jnp.abs(velocity) + root


def cell_sides(load, j):
    uppers, lowers = [], []
    for c in range(NF):
        here = load(c, j)
        delta = 0.25 * (load(c, j + 1) - load(c, j - 1))
        uppers.append(here + delta)
        lowers.append(here - delta)
    return uppers, lowers


def interface(left, left_flux, left_speed, right, right_flux, right_speed):
    widest = jnp.maximum(left_speed, right_speed)
    return [(left_flux[c] + right_flux[c]) - widest * (right[c] - left[c]) for c in range(NF)]


def body(fields, level, relation, half, near, sends, out, step_out,
         px, py, cx, cy, level_v, relation_v, half_v, near_v, sends_v,
         own, own0, far, far0, send, recv, edge, coarse, low, heard_z, heard_ends, heard_plane,
         edge_sem, load_sem, small_sem, bulk_send, bulk_recv, low_send, low_recv):
    me = lax.axis_index("patch")
    core = lax.rem(me, 2)
    z = lax.rem(me // 2, DIM_Z)
    x = lax.rem(me // (2 * DIM_Z), DIM_X)
    y = me // (2 * DIM_Z * DIM_X)
    total = DIM_Y * DIM_X * DIM_Z * 2

    def place(yy, xx, zz, cc):
        return ((yy * DIM_X + xx) * DIM_Z + zz) * 2 + cc

    def within(device):
        return jnp.logical_and(device >= 0, device < total)

    curve = [me + o for o in offsets()]
    sources = [me - o for o in offsets()]
    plane = [
        place(lax.rem(y + j, DIM_Y), lax.rem(x + k, DIM_X), z, cc)
        for j in range(DIM_Y) for k in range(DIM_X) for cc in (core, 1 - core)
    ][1:]
    steps_z = [k for k in range(-NEAR_Z, NEAR_Z + 1) if k]
    along_z = [place(y, x, lax.rem(z + k + DIM_Z, DIM_Z), core) for k in steps_z]
    ends_z = [along_z[0], along_z[-1]]

    barrier = pltpu.get_barrier_semaphore()
    expected = len(plane) + len(along_z)
    for partner in curve:
        expected = expected + within(partner).astype(jnp.int32)

        @pl.when(within(partner))
        def _():
            pl.semaphore_signal(barrier, inc=1, device_id=(partner,), device_id_type=MESH)

    for partner in along_z + plane:
        pl.semaphore_signal(barrier, inc=1, device_id=(partner,), device_id_type=MESH)

    smalls = [
        pltpu.make_async_copy(source, target, small_sem.at[n])
        for n, (source, target) in enumerate(
            [(sends, sends_v), (level, level_v), (relation, relation_v), (half, half_v), (near, near_v)]
        )
    ]
    edges = [
        pltpu.make_async_copy(
            fields.at[c, pl.ds(first, 4)], px.at[c, pl.ds(first + 2, 4)], edge_sem.at[2 * c + first // 28]
        )
        for c in range(NF) for first in (0, CELLS - 4)
    ]
    middles = [
        pltpu.make_async_copy(
            fields.at[c, pl.ds(4, CELLS - 8)], px.at[c, pl.ds(6, CELLS - 8)], load_sem.at[c]
        )
        for c in range(NF)
    ]
    for copy in smalls + edges + middles:
        copy.start()

    px2 = px.reshape(NF * PLANES * CELLS, LANES)
    py2 = py.reshape(NF * PLANES * CELLS, LANES)
    cy2 = cy.reshape(NF * CELLS * CELLS, LANES)
    out2 = out.reshape(NF * CELLS * CELLS, LANES)

    def restricted(ref, first, second):
        evens = ref[pl.ds(first, 16, stride=2), :] + ref[pl.ds(second, 16, stride=2), :]
        odds = ref[pl.ds(first + 1, 16, stride=2), :] + ref[pl.ds(second + 1, 16, stride=2), :]
        return 0.25 * (evens + odds)

    def pack(faces):
        for face in faces:
            planes = px2 if face < 2 else py2
            for c in range(NF):
                at = [(c * PLANES + (2 + k if face % 2 == 0 else 33 - k)) * CELLS for k in range(4)]
                row = (face * NF + c) * ROWS
                own[pl.ds(row, CELLS), :] = planes[pl.ds(at[0], CELLS), :]
                own[pl.ds(row + 32, CELLS), :] = planes[pl.ds(at[1], CELLS), :]
                own[pl.ds(row + 64, 16), :] = restricted(planes, at[2], at[3])
                own0[pl.ds((face * NF + c) * 16, 16), :] = restricted(planes, at[0], at[1])

    for copy in smalls + edges:
        copy.wait()
    pack((0, 1))

    lane = lax.broadcasted_iota(jnp.int32, (SEND, LANES), 1)
    slot = lax.broadcasted_iota(jnp.int32, (SEND, LANES), 0)
    listed = jnp.take_along_axis(jnp.concatenate([sends_v[...], jnp.zeros((SEND, LANES - NSLOT), jnp.int32)], axis=1), lane // SEND, axis=1)
    listed = jnp.sum(jnp.where(lax.rem(lane, SEND) == slot, listed, 0), axis=0, keepdims=True)
    listed = jnp.broadcast_to(listed, (LANES, LANES))
    def offer(tiles):
        for tile in tiles:
            columns = pl.ds(tile * LANES, LANES)
            send[:, columns] = jnp.take_along_axis(own[columns, :], listed, axis=1).T

    offer(range(5))
    for copy in middles:
        copy.wait()

    def scan_plane(i, best):
        state = [px[c, i + 2] for c in range(NF)]
        for c in range(NF):
            py2[pl.ds((c * PLANES + 2) * CELLS + i, CELLS, stride=CELLS), :] = state[c]
        inverse, root = wave(state[0])
        return jnp.maximum(best, jnp.maximum(jnp.abs(state[1]), jnp.abs(state[2])) * inverse + root)

    best = lax.fori_loop(0, CELLS, scan_plane, jnp.zeros((CELLS, LANES), F32), unroll=4)
    top_speed = jnp.max(best, axis=0, keepdims=True)
    spacing = lax.shift_left(jnp.ones((1, LANES), jnp.int32), 6 - level_v[...]).astype(F32)
    low[0] = spacing / top_speed

    def tell(value, targets, slots, stage):
        for n, target in enumerate(targets):
            pltpu.make_async_remote_copy(
                src_ref=value, dst_ref=slots.at[n], send_sem=low_send.at[stage], recv_sem=low_recv.at[stage],
                device_id=(target,), device_id_type=MESH,
            ).start()

    def hear(slots, stage):
        pltpu.make_async_copy(slots, slots, low_recv.at[stage]).wait()
        return jnp.min(slots[...], axis=0)

    def block_at(ref, part, k):
        return ref.at[pl.ds(k * SEND, SEND), pl.ds(PARTS[part][0] * LANES, PARTS[part][1] * LANES)]

    def exchange(part):
        for k in FAR_FIRST:

            @pl.when(within(curve[k]))
            def _():
                pltpu.make_async_remote_copy(
                    src_ref=block_at(send, part, k), dst_ref=block_at(recv, part, k), send_sem=bulk_send.at[k],
                    recv_sem=bulk_recv.at[part, k], device_id=(curve[k],), device_id_type=MESH,
                ).start()

    def arrived(part):
        for k in range(NSLOT):

            @pl.when(within(sources[k]))
            def _():
                block = block_at(recv, part, k)
                pltpu.make_async_copy(block, block, bulk_recv.at[part, k]).wait()

        first, count = PARTS[part]
        for tile in range(first, first + count):
            columns = pl.ds(tile * LANES, LANES)
            far[columns, :] = recv[:, columns].T

    pl.semaphore_wait(barrier, expected)
    tell(low.at[0], along_z, heard_z, 0)
    exchange(0)

    pack((2, 3))
    offer(range(5, 10))

    def interior(ref, normal, change):
        def row_tile(t, carry):
            rows = pl.ds(pl.multiple_of(t * 8, 8), 8)

            def load(c, j):
                return ref[c, j, rows, :]

            def advance(j, carried):
                left, left_flux, left_speed, before = carried
                upper, right = cell_sides(load, j + 1)
                right_flux, right_speed = physical(right, normal)
                flux = interface(left, left_flux, left_speed, right, right_flux, right_speed)
                for c in range(NF):
                    change[c, j - 2, rows, :] = flux[c] - before[c]
                upper_flux, upper_speed = physical(upper, normal)
                return upper, upper_flux, upper_speed, flux

            first, _ = cell_sides(load, 3)
            first_flux, first_speed = physical(first, normal)
            zero = jnp.zeros((8, LANES), F32)
            carried = advance(3, (first, first_flux, first_speed, [zero] * NF))
            last = lax.fori_loop(4, 32, advance, carried, unroll=4)
            for c in range(NF):
                change[c, 0, rows, :] = zero
                change[c, 30, rows, :] = -last[3][c]
                change[c, 31, rows, :] = zero
            return carry

        lax.fori_loop(0, 4, row_tile, 0)

    interior(px, 1, cx)

    low[1] = jnp.minimum(low[0], hear(heard_z, 0))
    tell(low.at[1], ends_z, heard_ends, 1)
    for part in (1, 2, 3):
        exchange(part)

    interior(py, 2, cy)

    low[2] = jnp.minimum(low[1], hear(heard_ends, 1))
    tell(low.at[2], plane, heard_plane, 2)

    def shallow(face):
        for c in range(NF):
            row = (face * NF + c) * ROWS
            far0[pl.ds((face * NF + c) * 16, 16), :] = restricted(far, row, row + 32)

    def pick(mine, theirs, row, count, index):
        spot = jnp.broadcast_to(lax.rem(index, LANES), (count, LANES))
        remote = jnp.broadcast_to(index, (count, LANES)) >= LANES
        return jnp.where(
            remote,
            jnp.take_along_axis(theirs[pl.ds(row, count), :], spot, axis=1),
            jnp.take_along_axis(mine[pl.ds(row, count), :], spot, axis=1),
        )

    def ghosts(face):
        planes = px if face < 2 else py
        opposite = face ^ 1
        kind = jnp.broadcast_to(relation_v[pl.ds(face, 1), :], (CELLS, LANES))
        upper = jnp.broadcast_to(half_v[pl.ds(face, 1), :], (16, LANES)) == 1
        first = near_v[face, pl.ds(0, 1), :]
        second = near_v[face, pl.ds(1, 1), :]
        for c in range(NF):
            row = (opposite * NF + c) * ROWS
            row0 = (opposite * NF + c) * 16
            level_same = [pick(own, far, row + 32 * g, CELLS, first) for g in range(2)]
            finer = [
                jnp.concatenate([pick(own0, far0, row0, 16, first), pick(own0, far0, row0, 16, second)], axis=0),
                jnp.concatenate([pick(own, far, row + 64, 16, first), pick(own, far, row + 64, 16, second)], axis=0),
            ]
            value = level_same[0]
            edge[pl.ds(8, CELLS), :] = value
            edge[pl.ds(7, 1), :] = value[0:1]
            edge[pl.ds(40, 1), :] = value[31:32]
            slope = edge[pl.ds(9, CELLS), :] - edge[pl.ds(7, CELLS), :]
            base = jnp.where(upper, value[16:], value[:16])
            lean = 0.125 * jnp.where(upper, slope[16:], slope[:16])
            coarse[pl.ds(0, 16, stride=2), :] = base - lean
            coarse[pl.ds(1, 16, stride=2), :] = base + lean
            wide = coarse[...]
            sign = -1.0 if c == 1 + face // 2 else 1.0
            for g in range(2):
                mirror = sign * own[pl.ds((face * NF + c) * ROWS + 32 * g, CELLS), :]
                ghost = jnp.where(
                    kind == 0,
                    mirror,
                    jnp.where(kind == 1, level_same[g], jnp.where(kind == 2, wide, finer[g])),
                )
                planes[c, 1 - g if face % 2 == 0 else 34 + g] = ghost

    def rim(ref, normal, face, apply):
        start = 1 if face % 2 == 0 else 32

        def load(c, j):
            return ref[c, j]

        sides = [cell_sides(load, j) for j in (start, start + 1, start + 2)]
        flux = []
        for n in range(2):
            left, right = sides[n][0], sides[n + 1][1]
            left_flux, left_speed = physical(left, normal)
            right_flux, right_speed = physical(right, normal)
            flux.append(interface(left, left_flux, left_speed, right, right_flux, right_speed))
        for c in range(NF):
            if face % 2 == 0:
                apply(c, 0, flux[1][c] - flux[0][c])
                apply(c, 1, -flux[1][c])
            else:
                apply(c, 30, flux[0][c])
                apply(c, 31, flux[1][c] - flux[0][c])

    def apply_x(c, i, change):
        cx[c, i] = cx[c, i] + change

    arrived(0)
    shallow(0)
    ghosts(1)
    rim(px, 1, 1, apply_x)
    arrived(1)
    shallow(1)
    ghosts(0)
    rim(px, 1, 0, apply_x)

    lowest = jnp.minimum(low[2], hear(heard_plane, 2))
    time_step = COURANT * jnp.min(lowest, axis=1, keepdims=True)
    step_out[...] = jnp.broadcast_to(time_step, (1, LANES))
    ratio = jnp.broadcast_to(0.5 * (time_step / spacing), (CELLS, LANES))

    def settle(i, carry):
        for c in range(NF):
            turned = cy2[pl.ds(c * CELLS * CELLS + i, CELLS, stride=CELLS), :]
            out[c, i] = px[c, i + 2] - ratio * (cx[c, i] + turned)
        return carry

    lax.fori_loop(0, CELLS, settle, 0, unroll=2)

    def apply_y(c, j, change):
        rows = pl.ds(c * CELLS * CELLS + j, CELLS, stride=CELLS)
        out2[rows, :] = out2[rows, :] - ratio * change

    for stage, slots in enumerate((heard_z, heard_ends, heard_plane)):
        pltpu.make_async_copy(slots, slots, low_send.at[stage]).wait()

    arrived(2)
    shallow(2)
    ghosts(3)
    rim(py, 2, 3, apply_y)
    arrived(3)
    shallow(3)
    ghosts(2)
    rim(py, 2, 2, apply_y)

    for k in range(NSLOT):

        @pl.when(within(curve[k]))
        def _():
            block = send.at[pl.ds(k * SEND, SEND)]
            pltpu.make_async_copy(block, block, bulk_send.at[k]).wait()


def on_device(fields, patch_level, relation, face_half, neighbour, send_list):
    any_space = pl.BlockSpec(memory_space=pl.ANY)
    vmem = pl.BlockSpec(memory_space=pltpu.VMEM)
    cube = (NF, CELLS, CELLS, LANES)
    advanced, step = pl.pallas_call(
        body,
        out_shape=(pltpu.VMEM(cube, F32), jax.ShapeDtypeStruct((1, LANES), F32)),
        in_specs=[any_space] * 6,
        out_specs=(vmem, vmem),
        scratch_shapes=[
            pltpu.VMEM((NF, PLANES, CELLS, LANES), F32),
            pltpu.VMEM((NF, PLANES, CELLS, LANES), F32),
            pltpu.VMEM(cube, F32),
            pltpu.VMEM(cube, F32),
            pltpu.VMEM((1, LANES), jnp.int32),
            pltpu.VMEM((4, LANES), jnp.int32),
            pltpu.VMEM((4, LANES), jnp.int32),
            pltpu.VMEM((4, 2, LANES), jnp.int32),
            pltpu.VMEM((SEND, NSLOT), jnp.int32),
            pltpu.VMEM((16 * ROWS, LANES), F32),
            pltpu.VMEM((256, LANES), F32),
            pltpu.VMEM((16 * ROWS, LANES), F32),
            pltpu.VMEM((256, LANES), F32),
            pltpu.VMEM((LANES, 16 * ROWS), F32),
            pltpu.VMEM((LANES, 16 * ROWS), F32),
            pltpu.VMEM((48, LANES), F32),
            pltpu.VMEM((CELLS, LANES), F32),
            pltpu.VMEM((3, 1, LANES), F32),
            pltpu.VMEM((2 * NEAR_Z, 1, LANES), F32),
            pltpu.VMEM((2, 1, LANES), F32),
            pltpu.VMEM((2 * DIM_X * DIM_Y - 1, 1, LANES), F32),
            pltpu.SemaphoreType.DMA((2 * NF,)),
            pltpu.SemaphoreType.DMA((NF,)),
            pltpu.SemaphoreType.DMA((5,)),
            pltpu.SemaphoreType.DMA((NSLOT,)),
            pltpu.SemaphoreType.DMA((len(PARTS), NSLOT)),
            pltpu.SemaphoreType.DMA((3,)),
            pltpu.SemaphoreType.DMA((3,)),
        ],
        compiler_params=pltpu.CompilerParams(collective_id=0, has_side_effects=True),
    )(
        fields,
        patch_level.reshape(1, LANES),
        relation.T,
        face_half.T,
        jnp.transpose(neighbour, (1, 2, 0)),
        send_list[0].T,
    )
    return advanced, step[0, 0]


def solution(mesh):
    return jax.shard_map(
        on_device,
        mesh=mesh,
        in_specs=(
            P(None, None, None, "patch"),
            P("patch"),
            P("patch", None),
            P("patch", None),
            P("patch", None, None),
            P("patch", None, None),
        ),
        out_specs=(P(None, None, None, "patch"), P()),
        check_vma=False,
    )
```

time: 50.1 us -> 39.9 us (0.80)
  Pallas kernels: 43.7 us -> 36.6 us
  local copies, waits for them, and re-layouts: 4.37 us -> 1.33 us
    pallas_call x1, Pallas kernels: 43.7 us -> 36.6 us  [on_device(): pl.pallas_call(body, out_shape=(pltpu.VMEM(cube, F32), jax.ShapeDtypeStru...]
    unnamed x3, local copies, waits for them, and re-layouts: 3.08 us -> 1.33 us
    pad x1 -> x0, local copies, waits for them, and re-layouts: 1.28 us -> none  [on_device(): jnp.pad(send_list[0].T, ((0, 0), (0, LANES - NSLOT)))]
where the time goes in v2:
time: 39.9 us; the launch traced here: 39.7 us
  Pallas kernels  36.6 us (92%)
  between operations  1.81 us (5%)
  local copies, waits for them, and re-layouts  1.33 us (3%)
    pallas_call x1, Pallas kernels, on_device(): pl.pallas_call(body, out_shape=(pltpu.VMEM(cube, F32), jax.ShapeDtypeStru...  36.6 us
    unnamed x3, local copies, waits for them, and re-layouts  1.33 us

profile of v2, /device:TPU:1, one launch (start us, length us, event | category | flops | bytes accessed | tf_op | source)
XLA Modules:
  0.0 39.7 jit_solution(4366844242501774065)
XLA Ops:
  0.6 36.6 %shard_map.77 = (f32[4,32,32,128]{3,2,1,0:T(8,128)S(1)}, f32[1,128]{1,0:T(1,128)}) custom-call(f32[4,32,32,128]{3,2,1,0:T(8,128)} %fields.1, s32[1,128]{1,0:T(1,128)} %bitcast.13, s32[4,128]{1,0:T(4,128)} %bitcast.11, s32[4,128]{1,0:T(4,128)} %bitcast.12, s32[4,2,128]{2,1,0:T(2,128)} %bitcast.9, s32[8,16]{1,0:T(8,128)} %bitcast.10), custom_call_target="tpu_custom_call" | custom-call | tf_op jit(solution)/shard_map/pallas_call | solution.py:378
  37.2 0.0 copy-start
  37.2 1.3 %copy.10 = f32[4,32,32,128]{3,2,1,0:T(8,128)} copy(f32[4,32,32,128]{3,2,1,0:T(8,128)S(1)} %get-tuple-element.6) | data formatting | bytes 4194304
  38.6 0.0 copy-done
Async XLA Ops:
  37.2 1.3 %copy-start = (f32[1,128]{1,0:T(1,128)S(1)}, f32[1,128]{1,0:T(1,128)}, u32[]{:S(2)}) copy-start(f32[1,128]{1,0:T(1,128)} %get-tuple-element.5) | copy-start | bytes 1540

commit v3 on v2

--- a/solution.py
+++ b/solution.py
@@ -14,7 +14,9 @@
 PLANES = CELLS + 4
 ROWS = 80
 NSLOT = 2 * HOPS
-PARTS = ((0, 3), (3, 2), (5, 3), (8, 2))
+PARTS = ((0, 3), (3, 2), (5, 2), (7, 2))
+TILES = 9
+REST = 32
 FAR_FIRST = [7, 15, 6, 14, 5, 13, 4, 12, 3, 11, 2, 10, 1, 9, 0, 8]
 DIM_Y, DIM_X, DIM_Z = 4, 4, 16
 NEAR_Z = 4
@@ -57,8 +59,8 @@
 
 def body(fields, level, relation, half, near, sends, out, step_out,
          px, py, cx, cy, level_v, relation_v, half_v, near_v, sends_v,
-         own, own0, far, far0, send, recv, edge, coarse, low, heard_z, heard_ends, heard_plane,
-         edge_sem, load_sem, small_sem, bulk_send, bulk_recv, low_send, low_recv):
+         own, own0, far, far0, lean, far_lean, spare, send, recv, rest_send, rest_recv, edge, coarse, low, heard_z, heard_ends, heard_plane,
+         edge_sem, load_sem, small_sem, bulk_send, bulk_recv, rest_sem_send, rest_sem_recv, low_send, low_recv):
     me = lax.axis_index("patch")
     core = lax.rem(me, 2)
     z = lax.rem(me // 2, DIM_Z)
@@ -117,7 +119,6 @@
 
     px2 = px.reshape(NF * PLANES * CELLS, LANES)
     py2 = py.reshape(NF * PLANES * CELLS, LANES)
-    cy2 = cy.reshape(NF * CELLS * CELLS, LANES)
     out2 = out.reshape(NF * CELLS * CELLS, LANES)
 
     def restricted(ref, first, second):
@@ -148,21 +149,41 @@
     def offer(tiles):
         for tile in tiles:
             columns = pl.ds(tile * LANES, LANES)
-            send[:, columns] = jnp.take_along_axis(own[columns, :], listed, axis=1).T
+            rows = own[columns, :] if tile < 5 else lean[pl.ds((tile - 5) * LANES, LANES), :]
+            send[:, columns] = jnp.take_along_axis(rows, listed, axis=1).T
+
+    def thin():
+        for face in (2, 3):
+            for c in range(NF):
+                row = (face * NF + c) * ROWS
+                for g in range(2):
+                    lean[pl.ds((face - 2) * 256 + (2 * c + g) * 28, 28), :] = own[pl.ds(row + 32 * g + 2, 28), :]
+                lean[pl.ds((face - 2) * 256 + 224 + 8 * c, 8), :] = own[pl.ds(row + 66, 8), :]
+                lean[pl.ds(512 + (face - 2) * 16 + 4 * c, 4), :] = own[pl.ds(row + 74, 4), :]
+
+    group = lax.broadcasted_iota(jnp.int32, (REST, LANES), 1) // REST
+
+    def offer_rest():
+        spare[...] = jnp.take_along_axis(lean[pl.ds(4 * LANES, LANES), :], listed, axis=1).T
+        merged = spare[pl.ds(0, REST, stride=4), :]
+        for j in range(1, 4):
+            merged = jnp.where(group == j, pltpu.roll(spare[pl.ds(j, REST, stride=4), :], j * REST, 1), merged)
+        rest_send[...] = merged
 
     offer(range(5))
     for copy in middles:
         copy.wait()
 
-    def scan_plane(i, best):
-        state = [px[c, i + 2] for c in range(NF)]
-        for c in range(NF):
-            py2[pl.ds((c * PLANES + 2) * CELLS + i, CELLS, stride=CELLS), :] = state[c]
+    def scan_block(n, best):
+        low_x, low_y = pl.multiple_of(n // 4 * 8, 8), pl.multiple_of(lax.rem(n, 4) * 8, 8)
+        state = [px[c, pl.ds(low_x + 2, 8), pl.ds(low_y, 8), :] for c in range(NF)]
+        for c in range(NF):
+            py[c, pl.ds(low_y + 2, 8), pl.ds(low_x, 8), :] = jnp.swapaxes(state[c], 0, 1)
         inverse, root = wave(state[0])
         return jnp.maximum(best, jnp.maximum(jnp.abs(state[1]), jnp.abs(state[2])) * inverse + root)
 
-    best = lax.fori_loop(0, CELLS, scan_plane, jnp.zeros((CELLS, LANES), F32), unroll=4)
-    top_speed = jnp.max(best, axis=0, keepdims=True)
+    best = lax.fori_loop(0, 16, scan_block, jnp.zeros((8, 8, LANES), F32))
+    top_speed = jnp.max(jnp.max(best, axis=0), axis=0, keepdims=True)
     spacing = lax.shift_left(jnp.ones((1, LANES), jnp.int32), 6 - level_v[...]).astype(F32)
     low[0] = spacing / top_speed
 
@@ -189,6 +210,12 @@
                     src_ref=block_at(send, part, k), dst_ref=block_at(recv, part, k), send_sem=bulk_send.at[k],
                     recv_sem=bulk_recv.at[part, k], device_id=(curve[k],), device_id_type=MESH,
                 ).start()
+                if part == 2:
+                    rows = pl.ds(2 * k, 2)
+                    pltpu.make_async_remote_copy(
+                        src_ref=rest_send.at[rows], dst_ref=rest_recv.at[rows], send_sem=rest_sem_send.at[k],
+                        recv_sem=rest_sem_recv.at[k], device_id=(curve[k],), device_id_type=MESH,
+                    ).start()
 
     def arrived(part):
         for k in range(NSLOT):
@@ -197,18 +224,30 @@
             def _():
                 block = block_at(recv, part, k)
                 pltpu.make_async_copy(block, block, bulk_recv.at[part, k]).wait()
+                if part == 2:
+                    block = rest_recv.at[pl.ds(2 * k, 2)]
+                    pltpu.make_async_copy(block, block, rest_sem_recv.at[k]).wait()
 
         first, count = PARTS[part]
         for tile in range(first, first + count):
             columns = pl.ds(tile * LANES, LANES)
-            far[columns, :] = recv[:, columns].T
+            if tile < 5:
+                far[columns, :] = recv[:, columns].T
+            else:
+                far_lean[pl.ds((tile - 5) * LANES, LANES), :] = recv[:, columns].T
+        if part == 2:
+            for j in range(4):
+                spare[pl.ds(j, REST, stride=4), :] = pltpu.roll(rest_recv[...], (LANES - j * REST) % LANES, 1)
+            far_lean[pl.ds(4 * LANES, LANES), :] = spare[...].T
 
     pl.semaphore_wait(barrier, expected)
     tell(low.at[0], along_z, heard_z, 0)
     exchange(0)
 
     pack((2, 3))
-    offer(range(5, 10))
+    thin()
+    offer(range(5, TILES))
+    offer_rest()
 
     def interior(ref, normal, change):
         def row_tile(t, carry):
@@ -240,17 +279,40 @@
 
         lax.fori_loop(0, 4, row_tile, 0)
 
-    interior(px, 1, cx)
-
     low[1] = jnp.minimum(low[0], hear(heard_z, 0))
     tell(low.at[1], ends_z, heard_ends, 1)
     for part in (1, 2, 3):
         exchange(part)
 
+    interior(px, 1, cx)
     interior(py, 2, cy)
 
     low[2] = jnp.minimum(low[1], hear(heard_ends, 1))
     tell(low.at[2], plane, heard_plane, 2)
+
+    def corners():
+        for face in (2, 3):
+            for c in range(NF):
+                row = (face * NF + c) * ROWS
+                west, east = c * ROWS, (NF + c) * ROWS
+                west0, east0 = c * 16, (NF + c) * 16
+                for g in range(2):
+                    side = g if face == 2 else 31 - g
+                    for t, source in ((0, west), (1, west + 32), (30, east + 32), (31, east)):
+                        far[pl.ds(row + 32 * g + t, 1), :] = far[pl.ds(source + side, 1), :]
+                side = 1 if face == 2 else 14
+                far[pl.ds(row + 64, 1), :] = far0[pl.ds(west0 + side, 1), :]
+                far[pl.ds(row + 65, 1), :] = far[pl.ds(west + 64 + side, 1), :]
+                far[pl.ds(row + 78, 1), :] = far[pl.ds(east + 64 + side, 1), :]
+                far[pl.ds(row + 79, 1), :] = far0[pl.ds(east0 + side, 1), :]
+
+    def fatten(face):
+        for c in range(NF):
+            row = (face * NF + c) * ROWS
+            for g in range(2):
+                far[pl.ds(row + 32 * g + 2, 28), :] = far_lean[pl.ds((face - 2) * 256 + (2 * c + g) * 28, 28), :]
+            far[pl.ds(row + 66, 8), :] = far_lean[pl.ds((face - 2) * 256 + 224 + 8 * c, 8), :]
+            far[pl.ds(row + 74, 4), :] = far_lean[pl.ds(512 + (face - 2) * 16 + 4 * c, 4), :]
 
     def shallow(face):
         for c in range(NF):
@@ -325,6 +387,16 @@
     def apply_x(c, i, change):
         cx[c, i] = cx[c, i] + change
 
+    def join(n, carry):
+        low_x, low_y = pl.multiple_of(n // 4 * 8, 8), pl.multiple_of(lax.rem(n, 4) * 8, 8)
+        for c in range(NF):
+            turned = jnp.swapaxes(cy[c, pl.ds(low_y, 8), pl.ds(low_x, 8), :], 0, 1)
+            at = (c, pl.ds(low_x, 8), pl.ds(low_y, 8))
+            cx[at] = cx[at] + turned
+        return carry
+
+    lax.fori_loop(0, 16, join, 0)
+
     arrived(0)
     shallow(0)
     ghosts(1)
@@ -333,6 +405,7 @@
     shallow(1)
     ghosts(0)
     rim(px, 1, 0, apply_x)
+    corners()
 
     lowest = jnp.minimum(low[2], hear(heard_plane, 2))
     time_step = COURANT * jnp.min(lowest, axis=1, keepdims=True)
@@ -341,8 +414,7 @@
 
     def settle(i, carry):
         for c in range(NF):
-            turned = cy2[pl.ds(c * CELLS * CELLS + i, CELLS, stride=CELLS), :]
-            out[c, i] = px[c, i + 2] - ratio * (cx[c, i] + turned)
+            out[c, i] = px[c, i + 2] - ratio * cx[c, i]
         return carry
 
     lax.fori_loop(0, CELLS, settle, 0, unroll=2)
@@ -355,10 +427,12 @@
         pltpu.make_async_copy(slots, slots, low_send.at[stage]).wait()
 
     arrived(2)
+    fatten(2)
     shallow(2)
     ghosts(3)
     rim(py, 2, 3, apply_y)
     arrived(3)
+    fatten(3)
     shallow(3)
     ghosts(2)
     rim(py, 2, 2, apply_y)
@@ -369,6 +443,24 @@
         def _():
             block = send.at[pl.ds(k * SEND, SEND)]
             pltpu.make_async_copy(block, block, bulk_send.at[k]).wait()
+            block = rest_send.at[pl.ds(2 * k, 2)]
+            pltpu.make_async_copy(block, block, rest_sem_send.at[k]).wait()
+
+
+def deliver(advanced, step, out, step_out, one, sem):
+    copies = [
+        pltpu.make_async_copy(
+            advanced.at[c, pl.ds(8 * n, 8)], out.at[c, pl.ds(8 * n, 8)], sem.at[4 * c + n]
+        )
+        for c in range(NF) for n in range(4)
+    ]
+    for copy in copies:
+        copy.start()
+    one[...] = step[:, pl.ds(0, 1)]
+    copies.append(pltpu.make_async_copy(one, step_out, sem.at[4 * NF]))
+    copies[-1].start()
+    for copy in copies:
+        copy.wait()
 
 
 def on_device(fields, patch_level, relation, face_half, neighbour, send_list):
@@ -377,7 +469,7 @@
     cube = (NF, CELLS, CELLS, LANES)
     advanced, step = pl.pallas_call(
         body,
-        out_shape=(pltpu.VMEM(cube, F32), jax.ShapeDtypeStruct((1, LANES), F32)),
+        out_shape=(pltpu.VMEM(cube, F32), pltpu.VMEM((1, LANES), F32)),
         in_specs=[any_space] * 6,
         out_specs=(vmem, vmem),
         scratch_shapes=[
@@ -394,8 +486,13 @@
             pltpu.VMEM((256, LANES), F32),
             pltpu.VMEM((16 * ROWS, LANES), F32),
             pltpu.VMEM((256, LANES), F32),
-            pltpu.VMEM((LANES, 16 * ROWS), F32),
-            pltpu.VMEM((LANES, 16 * ROWS), F32),
+            pltpu.VMEM((5 * LANES, LANES), F32),
+            pltpu.VMEM((5 * LANES, LANES), F32),
+            pltpu.VMEM((LANES, LANES), F32),
+            pltpu.VMEM((LANES, TILES * LANES), F32),
+            pltpu.VMEM((LANES, TILES * LANES), F32),
+            pltpu.VMEM((REST, LANES), F32),
+            pltpu.VMEM((REST, LANES), F32),
             pltpu.VMEM((48, LANES), F32),
             pltpu.VMEM((CELLS, LANES), F32),
             pltpu.VMEM((3, 1, LANES), F32),
@@ -407,6 +504,8 @@
             pltpu.SemaphoreType.DMA((5,)),
             pltpu.SemaphoreType.DMA((NSLOT,)),
             pltpu.SemaphoreType.DMA((len(PARTS), NSLOT)),
+            pltpu.SemaphoreType.DMA((NSLOT,)),
+            pltpu.SemaphoreType.DMA((NSLOT,)),
             pltpu.SemaphoreType.DMA((3,)),
             pltpu.SemaphoreType.DMA((3,)),
         ],
@@ -419,7 +518,17 @@
         jnp.transpose(neighbour, (1, 2, 0)),
         send_list[0].T,
     )
-    return advanced, step[0, 0]
+    advanced, step = pl.pallas_call(
+        deliver,
+        out_shape=(jax.ShapeDtypeStruct(cube, F32), jax.ShapeDtypeStruct((1, 1), F32)),
+        in_specs=[vmem, vmem],
+        out_specs=(any_space, any_space),
+        scratch_shapes=[pltpu.VMEM((1, 1), F32), pltpu.SemaphoreType.DMA((4 * NF + 1,))],
+    )(
+        pltpu.with_memory_space_constraint(advanced, pltpu.VMEM),
+        pltpu.with_memory_space_constraint(step, pltpu.VMEM),
+    )
+    return advanced, step.reshape(())
 
 
 def solution(mesh):

time: 39.9 us -> 36.9 us (0.925)
  the two profiles are of different devices: /device:TPU:1 before, /device:TPU:8 now
where the time goes in v3:
time: 36.9 us; the launch traced here: 36.8 us
  Pallas kernels  36.1 us (98%)
  between operations  0.64 us (2%)
    pallas_call x1, Pallas kernels, on_device(): pl.pallas_call(body, out_shape=(pltpu.VMEM(cube, F32), pltpu.VMEM((1, LAN...  34.7 us
    pallas_call x1, Pallas kernels, on_device(): pl.pallas_call(deliver, out_shape=(jax.ShapeDtypeStruct(cube, F32), jax.S...  1.45 us

profile of v3, /device:TPU:8, one launch (start us, length us, event | category | flops | bytes accessed | tf_op | source)
XLA Modules:
  0.0 36.8 jit_solution(15534918911188909865)
XLA Ops:
  0.6 34.7 %shard_map.77 = (f32[4,32,32,128]{3,2,1,0:T(8,128)S(1)}, f32[1,128]{1,0:T(1,128)S(1)}) custom-call(f32[4,32,32,128]{3,2,1,0:T(8,128)} %fields.1, s32[1,128]{1,0:T(1,128)} %bitcast.12, s32[4,128]{1,0:T(4,128)} %bitcast.10, s32[4,128]{1,0:T(4,128)} %bitcast.11, s32[4,2,128]{2,1,0:T(2,128)} %bitcast.8, s32[8,16]{1,0:T(8,128)} %bitcast.9), custom_call_target="tpu_custom_call" | custom-call | tf_op jit(solution)/shard_map/pallas_call | solution.py:470
  35.3 1.5 %shard_map.78 = (f32[4,32,32,128]{3,2,1,0:T(8,128)}, f32[1,1]{1,0:T(1,128)}) custom-call(f32[4,32,32,128]{3,2,1,0:T(8,128)S(1)} %get-tuple-element.6.advanced, f32[1,128]{1,0:T(1,128)S(1)} %get-tuple-element.7.step), custom_call_target="tpu_custom_call" | custom-call | tf_op jit(solution)/shard_map/pallas_call | solution.py:521

commit v4 on v3

--- a/solution.py
+++ b/solution.py
@@ -14,7 +14,7 @@
 PLANES = CELLS + 4
 ROWS = 80
 NSLOT = 2 * HOPS
-PARTS = ((0, 3), (3, 2), (5, 2), (7, 2))
+PARTS = ((0, 3), (3, 4), (7, 2))
 TILES = 9
 REST = 32
 FAR_FIRST = [7, 15, 6, 14, 5, 13, 4, 12, 3, 11, 2, 10, 1, 9, 0, 8]
@@ -60,7 +60,7 @@
 def body(fields, level, relation, half, near, sends, out, step_out,
          px, py, cx, cy, level_v, relation_v, half_v, near_v, sends_v,
          own, own0, far, far0, lean, far_lean, spare, send, recv, rest_send, rest_recv, edge, coarse, low, heard_z, heard_ends, heard_plane,
-         edge_sem, load_sem, small_sem, bulk_send, bulk_recv, rest_sem_send, rest_sem_recv, low_send, low_recv):
+         edge_sem, load_sem, small_sem, bulk_send, bulk_recv, rest_sem_send, rest_sem_recv, low_send, low_recv, round_sem):
     me = lax.axis_index("patch")
     core = lax.rem(me, 2)
     z = lax.rem(me // 2, DIM_Z)
@@ -80,12 +80,19 @@
         place(lax.rem(y + j, DIM_Y), lax.rem(x + k, DIM_X), z, cc)
         for j in range(DIM_Y) for k in range(DIM_X) for cc in (core, 1 - core)
     ][1:]
+    beside = [
+        place(y, lax.rem(x + 1, DIM_X), z, core),
+        place(y, lax.rem(x + DIM_X - 1, DIM_X), z, core),
+        place(lax.rem(y + 1, DIM_Y), x, z, core),
+        place(lax.rem(y + DIM_Y - 1, DIM_Y), x, z, core),
+        place(y, x, z, 1 - core),
+    ]
     steps_z = [k for k in range(-NEAR_Z, NEAR_Z + 1) if k]
     along_z = [place(y, x, lax.rem(z + k + DIM_Z, DIM_Z), core) for k in steps_z]
     ends_z = [along_z[0], along_z[-1]]
 
     barrier = pltpu.get_barrier_semaphore()
-    expected = len(plane) + len(along_z)
+    expected = len(beside) + len(along_z)
     for partner in curve:
         expected = expected + within(partner).astype(jnp.int32)
 
@@ -93,7 +100,7 @@
         def _():
             pl.semaphore_signal(barrier, inc=1, device_id=(partner,), device_id_type=MESH)
 
-    for partner in along_z + plane:
+    for partner in along_z + beside:
         pl.semaphore_signal(barrier, inc=1, device_id=(partner,), device_id_type=MESH)
 
     smalls = [
@@ -210,7 +217,7 @@
                     src_ref=block_at(send, part, k), dst_ref=block_at(recv, part, k), send_sem=bulk_send.at[k],
                     recv_sem=bulk_recv.at[part, k], device_id=(curve[k],), device_id_type=MESH,
                 ).start()
-                if part == 2:
+                if part == 1:
                     rows = pl.ds(2 * k, 2)
                     pltpu.make_async_remote_copy(
                         src_ref=rest_send.at[rows], dst_ref=rest_recv.at[rows], send_sem=rest_sem_send.at[k],
@@ -224,7 +231,7 @@
             def _():
                 block = block_at(recv, part, k)
                 pltpu.make_async_copy(block, block, bulk_recv.at[part, k]).wait()
-                if part == 2:
+                if part == 1:
                     block = rest_recv.at[pl.ds(2 * k, 2)]
                     pltpu.make_async_copy(block, block, rest_sem_recv.at[k]).wait()
 
@@ -235,19 +242,29 @@
                 far[columns, :] = recv[:, columns].T
             else:
                 far_lean[pl.ds((tile - 5) * LANES, LANES), :] = recv[:, columns].T
-        if part == 2:
+        if part == 1:
             for j in range(4):
                 spare[pl.ds(j, REST, stride=4), :] = pltpu.roll(rest_recv[...], (LANES - j * REST) % LANES, 1)
             far_lean[pl.ds(4 * LANES, LANES), :] = spare[...].T
 
+    def relay(n):
+        for partner in beside:
+            pl.semaphore_signal(round_sem.at[n], inc=1, device_id=(partner,), device_id_type=MESH)
+
+    def relayed(n):
+        pl.semaphore_wait(round_sem.at[n], len(beside))
+
     pl.semaphore_wait(barrier, expected)
     tell(low.at[0], along_z, heard_z, 0)
     exchange(0)
+    relay(0)
 
     pack((2, 3))
     thin()
     offer(range(5, TILES))
     offer_rest()
+    relayed(0)
+    relay(1)
 
     def interior(ref, normal, change):
         def row_tile(t, carry):
@@ -281,13 +298,18 @@
 
     low[1] = jnp.minimum(low[0], hear(heard_z, 0))
     tell(low.at[1], ends_z, heard_ends, 1)
-    for part in (1, 2, 3):
+    for part in (1, 2):
         exchange(part)
+    relayed(1)
+    relay(2)
 
     interior(px, 1, cx)
+    relayed(2)
+    relay(3)
     interior(py, 2, cy)
 
     low[2] = jnp.minimum(low[1], hear(heard_ends, 1))
+    relayed(3)
     tell(low.at[2], plane, heard_plane, 2)
 
     def corners():
@@ -401,17 +423,17 @@
     shallow(0)
     ghosts(1)
     rim(px, 1, 1, apply_x)
+    lowest = jnp.minimum(low[2], hear(heard_plane, 2))
+    time_step = COURANT * jnp.min(lowest, axis=1, keepdims=True)
+    step_out[...] = jnp.broadcast_to(time_step, (1, LANES))
+    ratio = jnp.broadcast_to(0.5 * (time_step / spacing), (CELLS, LANES))
+
     arrived(1)
     shallow(1)
     ghosts(0)
     rim(px, 1, 0, apply_x)
     corners()
 
-    lowest = jnp.minimum(low[2], hear(heard_plane, 2))
-    time_step = COURANT * jnp.min(lowest, axis=1, keepdims=True)
-    step_out[...] = jnp.broadcast_to(time_step, (1, LANES))
-    ratio = jnp.broadcast_to(0.5 * (time_step / spacing), (CELLS, LANES))
-
     def settle(i, carry):
         for c in range(NF):
             out[c, i] = px[c, i + 2] - ratio * cx[c, i]
@@ -426,12 +448,11 @@
     for stage, slots in enumerate((heard_z, heard_ends, heard_plane)):
         pltpu.make_async_copy(slots, slots, low_send.at[stage]).wait()
 
-    arrived(2)
     fatten(2)
     shallow(2)
     ghosts(3)
     rim(py, 2, 3, apply_y)
-    arrived(3)
+    arrived(2)
     fatten(3)
     shallow(3)
     ghosts(2)
@@ -450,14 +471,14 @@
 def deliver(advanced, step, out, step_out, one, sem):
     copies = [
         pltpu.make_async_copy(
-            advanced.at[c, pl.ds(8 * n, 8)], out.at[c, pl.ds(8 * n, 8)], sem.at[4 * c + n]
+            advanced.at[c, pl.ds(32 * n, 32)], out.at[c, pl.ds(32 * n, 32)], sem.at[1 * c + n]
         )
-        for c in range(NF) for n in range(4)
+        for c in range(NF) for n in range(1)
     ]
     for copy in copies:
         copy.start()
     one[...] = step[:, pl.ds(0, 1)]
-    copies.append(pltpu.make_async_copy(one, step_out, sem.at[4 * NF]))
+    copies.append(pltpu.make_async_copy(one, step_out, sem.at[1 * NF]))
     copies[-1].start()
     for copy in copies:
         copy.wait()
@@ -508,6 +529,7 @@
             pltpu.SemaphoreType.DMA((NSLOT,)),
             pltpu.SemaphoreType.DMA((3,)),
             pltpu.SemaphoreType.DMA((3,)),
+            pltpu.SemaphoreType.REGULAR((4,)),
         ],
         compiler_params=pltpu.CompilerParams(collective_id=0, has_side_effects=True),
     )(
@@ -523,7 +545,7 @@
         out_shape=(jax.ShapeDtypeStruct(cube, F32), jax.ShapeDtypeStruct((1, 1), F32)),
         in_specs=[vmem, vmem],
         out_specs=(any_space, any_space),
-        scratch_shapes=[pltpu.VMEM((1, 1), F32), pltpu.SemaphoreType.DMA((4 * NF + 1,))],
+        scratch_shapes=[pltpu.VMEM((1, 1), F32), pltpu.SemaphoreType.DMA((1 * NF + 1,))],
     )(
         pltpu.with_memory_space_constraint(advanced, pltpu.VMEM),
         pltpu.with_memory_space_constraint(step, pltpu.VMEM),

time: 36.9 us -> 36.3 us (0.984)
  the two profiles are of different devices: /device:TPU:8 before, /device:TPU:1 now
where the time goes in v4:
time: 36.3 us; the launch traced here: 36.1 us
  Pallas kernels  35.5 us (98%)
  between operations  0.64 us (2%)
    pallas_call x1, Pallas kernels, on_device(): pl.pallas_call(body, out_shape=(pltpu.VMEM(cube, F32), pltpu.VMEM((1, LAN...  34.1 us
    pallas_call x1, Pallas kernels, on_device(): pl.pallas_call(deliver, out_shape=(jax.ShapeDtypeStruct(cube, F32), jax.S...  1.36 us

profile of v4, /device:TPU:1, one launch (start us, length us, event | category | flops | bytes accessed | tf_op | source)
XLA Modules:
  0.0 36.1 jit_solution(5014410037867637954)
XLA Ops:
  0.6 34.1 %shard_map.77 = (f32[4,32,32,128]{3,2,1,0:T(8,128)S(1)}, f32[1,128]{1,0:T(1,128)S(1)}) custom-call(f32[4,32,32,128]{3,2,1,0:T(8,128)} %fields.1, s32[1,128]{1,0:T(1,128)} %bitcast.12, s32[4,128]{1,0:T(4,128)} %bitcast.10, s32[4,128]{1,0:T(4,128)} %bitcast.11, s32[4,2,128]{2,1,0:T(2,128)} %bitcast.8, s32[8,16]{1,0:T(8,128)} %bitcast.9), custom_call_target="tpu_custom_call" | custom-call | tf_op jit(solution)/shard_map/pallas_call | solution.py:491
  34.8 1.4 %shard_map.78 = (f32[4,32,32,128]{3,2,1,0:T(8,128)}, f32[1,1]{1,0:T(1,128)}) custom-call(f32[4,32,32,128]{3,2,1,0:T(8,128)S(1)} %get-tuple-element.6.advanced, f32[1,128]{1,0:T(1,128)S(1)} %get-tuple-element.7.step), custom_call_target="tpu_custom_call" | custom-call | tf_op jit(solution)/shard_map/pallas_call | solution.py:543

commit v5 on v4

--- a/solution.py
+++ b/solution.py
@@ -127,6 +127,7 @@
     px2 = px.reshape(NF * PLANES * CELLS, LANES)
     py2 = py.reshape(NF * PLANES * CELLS, LANES)
     out2 = out.reshape(NF * CELLS * CELLS, LANES)
+    cx2 = cx.reshape(NF * CELLS * CELLS, LANES)
 
     def restricted(ref, first, second):
         evens = ref[pl.ds(first, 16, stride=2), :] + ref[pl.ds(second, 16, stride=2), :]
@@ -423,40 +424,44 @@
     shallow(0)
     ghosts(1)
     rim(px, 1, 1, apply_x)
-    lowest = jnp.minimum(low[2], hear(heard_plane, 2))
-    time_step = COURANT * jnp.min(lowest, axis=1, keepdims=True)
-    step_out[...] = jnp.broadcast_to(time_step, (1, LANES))
-    ratio = jnp.broadcast_to(0.5 * (time_step / spacing), (CELLS, LANES))
+    def apply_y(c, j, change):
+        rows = pl.ds(c * CELLS * CELLS + j, CELLS, stride=CELLS)
+        cx2[rows, :] = cx2[rows, :] + change
 
     arrived(1)
     shallow(1)
     ghosts(0)
     rim(px, 1, 0, apply_x)
     corners()
-
-    def settle(i, carry):
-        for c in range(NF):
-            out[c, i] = px[c, i + 2] - ratio * cx[c, i]
-        return carry
-
-    lax.fori_loop(0, CELLS, settle, 0, unroll=2)
-
-    def apply_y(c, j, change):
-        rows = pl.ds(c * CELLS * CELLS + j, CELLS, stride=CELLS)
-        out2[rows, :] = out2[rows, :] - ratio * change
-
-    for stage, slots in enumerate((heard_z, heard_ends, heard_plane)):
-        pltpu.make_async_copy(slots, slots, low_send.at[stage]).wait()
-
     fatten(2)
     shallow(2)
     ghosts(3)
     rim(py, 2, 3, apply_y)
+
+    lowest = jnp.minimum(low[2], hear(heard_plane, 2))
+    time_step = COURANT * jnp.min(lowest, axis=1, keepdims=True)
+    step_out[...] = jnp.broadcast_to(time_step, (1, LANES))
+    ratio = jnp.broadcast_to(0.5 * (time_step / spacing), (CELLS, LANES))
+
+    def settle(i, carry):
+        for c in range(NF):
+            out[c, i] = px[c, i + 2] - ratio * cx[c, i]
+        return carry
+
+    lax.fori_loop(0, CELLS, settle, 0, unroll=2)
+
+    for stage, slots in enumerate((heard_z, heard_ends, heard_plane)):
+        pltpu.make_async_copy(slots, slots, low_send.at[stage]).wait()
+
+    def settled_y(c, j, change):
+        rows = pl.ds(c * CELLS * CELLS + j, CELLS, stride=CELLS)
+        out2[rows, :] = out2[rows, :] - ratio * change
+
     arrived(2)
     fatten(3)
     shallow(3)
     ghosts(2)
-    rim(py, 2, 2, apply_y)
+    rim(py, 2, 2, settled_y)
 
     for k in range(NSLOT):
 

time: 36.3 us -> 35.6 us (0.981)
  Pallas kernels: 35.5 us -> 34.5 us
    pallas_call x1, Pallas kernels: 34.1 us -> 33.2 us  [on_device(): pl.pallas_call(body, out_shape=(pltpu.VMEM(cube, F32), pltpu.VMEM((1, LAN...]
where the time goes in v5:
time: 35.6 us; the launch traced here: 35.2 us
  Pallas kernels  34.5 us (97%)
  between operations  0.64 us (2%)
    pallas_call x1, Pallas kernels, on_device(): pl.pallas_call(body, out_shape=(pltpu.VMEM(cube, F32), pltpu.VMEM((1, LAN...  33.2 us
    pallas_call x1, Pallas kernels, on_device(): pl.pallas_call(deliver, out_shape=(jax.ShapeDtypeStruct(cube, F32), jax.S...  1.36 us

profile of v5, /device:TPU:1, one launch (start us, length us, event | category | flops | bytes accessed | tf_op | source)
XLA Modules:
  0.0 35.2 jit_solution(9399693075387109976)
XLA Ops:
  0.6 33.2 %shard_map.77 = (f32[4,32,32,128]{3,2,1,0:T(8,128)S(1)}, f32[1,128]{1,0:T(1,128)S(1)}) custom-call(f32[4,32,32,128]{3,2,1,0:T(8,128)} %fields.1, s32[1,128]{1,0:T(1,128)} %bitcast.12, s32[4,128]{1,0:T(4,128)} %bitcast.10, s32[4,128]{1,0:T(4,128)} %bitcast.11, s32[4,2,128]{2,1,0:T(2,128)} %bitcast.8, s32[8,16]{1,0:T(8,128)} %bitcast.9), custom_call_target="tpu_custom_call" | custom-call | tf_op jit(solution)/shard_map/pallas_call | solution.py:496
  33.8 1.4 %shard_map.78 = (f32[4,32,32,128]{3,2,1,0:T(8,128)}, f32[1,1]{1,0:T(1,128)}) custom-call(f32[4,32,32,128]{3,2,1,0:T(8,128)S(1)} %get-tuple-element.6.advanced, f32[1,128]{1,0:T(1,128)S(1)} %get-tuple-element.7.step), custom_call_target="tpu_custom_call" | custom-call | tf_op jit(solution)/shard_map/pallas_call | solution.py:548

commit v6 on v5

v6 whole, which is shorter than its diff:
```python
import jax
import jax.numpy as jnp
from jax import lax
from jax.experimental import pallas as pl
from jax.experimental.pallas import tpu as pltpu
from jax.sharding import PartitionSpec as P

MESH = pl.DeviceIdType.MESH
CELLS = 32
NF = 4
LANES = 128
HOPS = 8
SEND = 8
PLANES = CELLS + 4
ROWS = 80
NSLOT = 2 * HOPS
PARTS = ((0, 3), (3, 4), (7, 2))
TILES = 9
REST = 32
FAR_FIRST = [7, 15, 6, 14, 5, 13, 4, 12, 3, 11, 2, 10, 1, 9, 0, 8]
DIM_Y, DIM_X, DIM_Z = 4, 4, 16
NEAR_Z = 4
COURANT = 0.4
F32 = jnp.float32


def offsets():
    return [k + 1 for k in range(HOPS)] + [-(k + 1) for k in range(HOPS)]


def wave(depth):
    r = lax.rsqrt(depth)
    return r * r, depth * r


def physical(state, normal):
    inverse, root = wave(state[0])
    momentum = state[normal]
    velocity = momentum * inverse
    flux = [momentum, state[1] * velocity, state[2] * velocity, state[3] * velocity]
    flux[normal] = flux[normal] + 0.5 * (state[0] * state[0])
    return flux, jnp.abs(velocity) + root


def cell_sides(load, j):
    uppers, lowers = [], []
    for c in range(NF):
        here = load(c, j)
        delta = 0.25 * (load(c, j + 1) - load(c, j - 1))
        uppers.append(here + delta)
        lowers.append(here - delta)
    return uppers, lowers


def interface(left, left_flux, left_speed, right, right_flux, right_speed):
    widest = jnp.maximum(left_speed, right_speed)
    return [(left_flux[c] + right_flux[c]) - widest * (right[c] - left[c]) for c in range(NF)]


def ghost_maker(own, own0, far, far0, relation_v, half_v, near_v, edge, coarse):
    def pick(mine, theirs, row, count, index):
        spot = jnp.broadcast_to(lax.rem(index, LANES), (count, LANES))
        remote = jnp.broadcast_to(index, (count, LANES)) >= LANES
        return jnp.where(
            remote,
            jnp.take_along_axis(theirs[pl.ds(row, count), :], spot, axis=1),
            jnp.take_along_axis(mine[pl.ds(row, count), :], spot, axis=1),
        )

    def ghosts(face, store):
        opposite = face ^ 1
        kind = jnp.broadcast_to(relation_v[pl.ds(face, 1), :], (CELLS, LANES))
        upper = jnp.broadcast_to(half_v[pl.ds(face, 1), :], (16, LANES)) == 1
        first = near_v[face, pl.ds(0, 1), :]
        second = near_v[face, pl.ds(1, 1), :]
        for c in range(NF):
            row = (opposite * NF + c) * ROWS
            row0 = (opposite * NF + c) * 16
            level_same = [pick(own, far, row + 32 * g, CELLS, first) for g in range(2)]
            finer = [
                jnp.concatenate([pick(own0, far0, row0, 16, first), pick(own0, far0, row0, 16, second)], axis=0),
                jnp.concatenate([pick(own, far, row + 64, 16, first), pick(own, far, row + 64, 16, second)], axis=0),
            ]
            value = level_same[0]
            edge[pl.ds(8, CELLS), :] = value
            edge[pl.ds(7, 1), :] = value[0:1]
            edge[pl.ds(40, 1), :] = value[31:32]
            slope = edge[pl.ds(9, CELLS), :] - edge[pl.ds(7, CELLS), :]
            base = jnp.where(upper, value[16:], value[:16])
            lean = 0.125 * jnp.where(upper, slope[16:], slope[:16])
            coarse[pl.ds(0, 16, stride=2), :] = base - lean
            coarse[pl.ds(1, 16, stride=2), :] = base + lean
            wide = coarse[...]
            sign = -1.0 if c == 1 + face // 2 else 1.0
            for g in range(2):
                mirror = sign * own[pl.ds((face * NF + c) * ROWS + 32 * g, CELLS), :]
                ghost = jnp.where(
                    kind == 0,
                    mirror,
                    jnp.where(kind == 1, level_same[g], jnp.where(kind == 2, wide, finer[g])),
                )
                store(c, 1 - g if face % 2 == 0 else 34 + g, ghost)

    return ghosts


def rim(load, normal, face, apply):
    start = 1 if face % 2 == 0 else 32

    sides = [cell_sides(load, j) for j in (start, start + 1, start + 2)]
    flux = []
    for n in range(2):
        left, right = sides[n][0], sides[n + 1][1]
        left_flux, left_speed = physical(left, normal)
        right_flux, right_speed = physical(right, normal)
        flux.append(interface(left, left_flux, left_speed, right, right_flux, right_speed))
    for c in range(NF):
        if face % 2 == 0:
            apply(c, 0, flux[1][c] - flux[0][c])
            apply(c, 1, -flux[1][c])
        else:
            apply(c, 30, flux[0][c])
            apply(c, 31, flux[1][c] - flux[0][c])


def body(fields, level, relation, half, near, sends,
         out, step_out, ratio_out, py, own, own0, far, far0, relation_v, half_v, near_v,
         px, cx, cy, level_v, sends_v, lean, far_lean, spare, send, recv, rest_send, rest_recv, edge, coarse, low, heard_z, heard_ends, heard_plane,
         edge_sem, load_sem, small_sem, bulk_send, bulk_recv, rest_sem_send, rest_sem_recv, low_send, low_recv, round_sem):
    me = lax.axis_index("patch")
    core = lax.rem(me, 2)
    z = lax.rem(me // 2, DIM_Z)
    x = lax.rem(me // (2 * DIM_Z), DIM_X)
    y = me // (2 * DIM_Z * DIM_X)
    total = DIM_Y * DIM_X * DIM_Z * 2

    def place(yy, xx, zz, cc):
        return ((yy * DIM_X + xx) * DIM_Z + zz) * 2 + cc

    def within(device):
        return jnp.logical_and(device >= 0, device < total)

    curve = [me + o for o in offsets()]
    sources = [me - o for o in offsets()]
    plane = [
        place(lax.rem(y + j, DIM_Y), lax.rem(x + k, DIM_X), z, cc)
        for j in range(DIM_Y) for k in range(DIM_X) for cc in (core, 1 - core)
    ][1:]
    beside = [
        place(y, lax.rem(x + 1, DIM_X), z, core),
        place(y, lax.rem(x + DIM_X - 1, DIM_X), z, core),
        place(lax.rem(y + 1, DIM_Y), x, z, core),
        place(lax.rem(y + DIM_Y - 1, DIM_Y), x, z, core),
        place(y, x, z, 1 - core),
    ]
    steps_z = [k for k in range(-NEAR_Z, NEAR_Z + 1) if k]
    along_z = [place(y, x, lax.rem(z + k + DIM_Z, DIM_Z), core) for k in steps_z]
    ends_z = [along_z[0], along_z[-1]]

    barrier = pltpu.get_barrier_semaphore()
    expected = len(beside) + len(along_z)
    for partner in curve:
        expected = expected + within(partner).astype(jnp.int32)

        @pl.when(within(partner))
        def _():
            pl.semaphore_signal(barrier, inc=1, device_id=(partner,), device_id_type=MESH)

    for partner in along_z + beside:
        pl.semaphore_signal(barrier, inc=1, device_id=(partner,), device_id_type=MESH)

    smalls = [
        pltpu.make_async_copy(source, target, small_sem.at[n])
        for n, (source, target) in enumerate(
            [(sends, sends_v), (level, level_v), (relation, relation_v), (half, half_v), (near, near_v)]
        )
    ]
    edges = [
        pltpu.make_async_copy(
            fields.at[c, pl.ds(first, 4)], px.at[c, pl.ds(first + 2, 4)], edge_sem.at[2 * c + first // 28]
        )
        for c in range(NF) for first in (0, CELLS - 4)
    ]
    middles = [
        pltpu.make_async_copy(
            fields.at[c, pl.ds(4, CELLS - 8)], px.at[c, pl.ds(6, CELLS - 8)], load_sem.at[c]
        )
        for c in range(NF)
    ]
    for copy in smalls + edges + middles:
        copy.start()

    px2 = px.reshape(NF * PLANES * CELLS, LANES)
    py2 = py.reshape(NF * PLANES * CELLS, LANES)
    cx2 = cx.reshape(NF * CELLS * CELLS, LANES)

    def restricted(ref, first, second):
        evens = ref[pl.ds(first, 16, stride=2), :] + ref[pl.ds(second, 16, stride=2), :]
        odds = ref[pl.ds(first + 1, 16, stride=2), :] + ref[pl.ds(second + 1, 16, stride=2), :]
        return 0.25 * (evens + odds)

    def pack(faces):
        for face in faces:
            planes = px2 if face < 2 else py2
            for c in range(NF):
                at = [(c * PLANES + (2 + k if face % 2 == 0 else 33 - k)) * CELLS for k in range(4)]
                row = (face * NF + c) * ROWS
                own[pl.ds(row, CELLS), :] = planes[pl.ds(at[0], CELLS), :]
                own[pl.ds(row + 32, CELLS), :] = planes[pl.ds(at[1], CELLS), :]
                own[pl.ds(row + 64, 16), :] = restricted(planes, at[2], at[3])
                own0[pl.ds((face * NF + c) * 16, 16), :] = restricted(planes, at[0], at[1])

    for copy in smalls + edges:
        copy.wait()
    pack((0, 1))

    lane = lax.broadcasted_iota(jnp.int32, (SEND, LANES), 1)
    slot = lax.broadcasted_iota(jnp.int32, (SEND, LANES), 0)
    listed = jnp.take_along_axis(jnp.concatenate([sends_v[...], jnp.zeros((SEND, LANES - NSLOT), jnp.int32)], axis=1), lane // SEND, axis=1)
    listed = jnp.sum(jnp.where(lax.rem(lane, SEND) == slot, listed, 0), axis=0, keepdims=True)
    listed = jnp.broadcast_to(listed, (LANES, LANES))
    def offer(tiles):
        for tile in tiles:
            columns = pl.ds(tile * LANES, LANES)
            rows = own[columns, :] if tile < 5 else lean[pl.ds((tile - 5) * LANES, LANES), :]
            send[:, columns] = jnp.take_along_axis(rows, listed, axis=1).T

    def thin():
        for face in (2, 3):
            for c in range(NF):
                row = (face * NF + c) * ROWS
                for g in range(2):
                    lean[pl.ds((face - 2) * 256 + (2 * c + g) * 28, 28), :] = own[pl.ds(row + 32 * g + 2, 28), :]
                lean[pl.ds((face - 2) * 256 + 224 + 8 * c, 8), :] = own[pl.ds(row + 66, 8), :]
                lean[pl.ds(512 + (face - 2) * 16 + 4 * c, 4), :] = own[pl.ds(row + 74, 4), :]

    group = lax.broadcasted_iota(jnp.int32, (REST, LANES), 1) // REST

    def offer_rest():
        spare[...] = jnp.take_along_axis(lean[pl.ds(4 * LANES, LANES), :], listed, axis=1).T
        merged = spare[pl.ds(0, REST, stride=4), :]
        for j in range(1, 4):
            merged = jnp.where(group == j, pltpu.roll(spare[pl.ds(j, REST, stride=4), :], j * REST, 1), merged)
        rest_send[...] = merged

    offer(range(5))
    for copy in middles:
        copy.wait()

    def scan_block(n, best):
        low_x, low_y = pl.multiple_of(n // 4 * 8, 8), pl.multiple_of(lax.rem(n, 4) * 8, 8)
        state = [px[c, pl.ds(low_x + 2, 8), pl.ds(low_y, 8), :] for c in range(NF)]
        for c in range(NF):
            py[c, pl.ds(low_y + 2, 8), pl.ds(low_x, 8), :] = jnp.swapaxes(state[c], 0, 1)
        inverse, root = wave(state[0])
        return jnp.maximum(best, jnp.maximum(jnp.abs(state[1]), jnp.abs(state[2])) * inverse + root)

    best = lax.fori_loop(0, 16, scan_block, jnp.zeros((8, 8, LANES), F32))
    top_speed = jnp.max(jnp.max(best, axis=0), axis=0, keepdims=True)
    spacing = lax.shift_left(jnp.ones((1, LANES), jnp.int32), 6 - level_v[...]).astype(F32)
    low[0] = spacing / top_speed

    def tell(value, targets, slots, stage):
        for n, target in enumerate(targets):
            pltpu.make_async_remote_copy(
                src_ref=value, dst_ref=slots.at[n], send_sem=low_send.at[stage], recv_sem=low_recv.at[stage],
                device_id=(target,), device_id_type=MESH,
            ).start()

    def hear(slots, stage):
        pltpu.make_async_copy(slots, slots, low_recv.at[stage]).wait()
        return jnp.min(slots[...], axis=0)

    def block_at(ref, part, k):
        return ref.at[pl.ds(k * SEND, SEND), pl.ds(PARTS[part][0] * LANES, PARTS[part][1] * LANES)]

    def exchange(part):
        for k in FAR_FIRST:

            @pl.when(within(curve[k]))
            def _():
                pltpu.make_async_remote_copy(
                    src_ref=block_at(send, part, k), dst_ref=block_at(recv, part, k), send_sem=bulk_send.at[k],
                    recv_sem=bulk_recv.at[part, k], device_id=(curve[k],), device_id_type=MESH,
                ).start()
                if part == 1:
                    rows = pl.ds(2 * k, 2)
                    pltpu.make_async_remote_copy(
                        src_ref=rest_send.at[rows], dst_ref=rest_recv.at[rows], send_sem=rest_sem_send.at[k],
                        recv_sem=rest_sem_recv.at[k], device_id=(curve[k],), device_id_type=MESH,
                    ).start()

    def arrived(part):
        for k in range(NSLOT):

            @pl.when(within(sources[k]))
            def _():
                block = block_at(recv, part, k)
                pltpu.make_async_copy(block, block, bulk_recv.at[part, k]).wait()
                if part == 1:
                    block = rest_recv.at[pl.ds(2 * k, 2)]
                    pltpu.make_async_copy(block, block, rest_sem_recv.at[k]).wait()

        first, count = PARTS[part]
        for tile in range(first, first + count):
            columns = pl.ds(tile * LANES, LANES)
            if tile < 5:
                far[columns, :] = recv[:, columns].T
            else:
                far_lean[pl.ds((tile - 5) * LANES, LANES), :] = recv[:, columns].T
        if part == 1:
            for j in range(4):
                spare[pl.ds(j, REST, stride=4), :] = pltpu.roll(rest_recv[...], (LANES - j * REST) % LANES, 1)
            far_lean[pl.ds(4 * LANES, LANES), :] = spare[...].T

    def relay(n):
        for partner in beside:
            pl.semaphore_signal(round_sem.at[n], inc=1, device_id=(partner,), device_id_type=MESH)

    def relayed(n):
        pl.semaphore_wait(round_sem.at[n], len(beside))

    pl.semaphore_wait(barrier, expected)
    tell(low.at[0], along_z, heard_z, 0)
    exchange(0)
    relay(0)

    pack((2, 3))
    thin()
    offer(range(5, TILES))
    offer_rest()
    relayed(0)
    relay(1)

    def interior(ref, normal, change):
        def row_tile(t, carry):
            rows = pl.ds(pl.multiple_of(t * 8, 8), 8)

            def load(c, j):
                return ref[c, j, rows, :]

            def advance(j, carried):
                left, left_flux, left_speed, before = carried
                upper, right = cell_sides(load, j + 1)
                right_flux, right_speed = physical(right, normal)
                flux = interface(left, left_flux, left_speed, right, right_flux, right_speed)
                for c in range(NF):
                    change[c, j - 2, rows, :] = flux[c] - before[c]
                upper_flux, upper_speed = physical(upper, normal)
                return upper, upper_flux, upper_speed, flux

            first, _ = cell_sides(load, 3)
            first_flux, first_speed = physical(first, normal)
            zero = jnp.zeros((8, LANES), F32)
            carried = advance(3, (first, first_flux, first_speed, [zero] * NF))
            last = lax.fori_loop(4, 32, advance, carried, unroll=4)
            for c in range(NF):
                change[c, 0, rows, :] = zero
                change[c, 30, rows, :] = -last[3][c]
                change[c, 31, rows, :] = zero
            return carry

        lax.fori_loop(0, 4, row_tile, 0)

    low[1] = jnp.minimum(low[0], hear(heard_z, 0))
    tell(low.at[1], ends_z, heard_ends, 1)
    for part in (1, 2):
        exchange(part)
    relayed(1)
    relay(2)

    interior(px, 1, cx)
    relayed(2)
    relay(3)
    interior(py, 2, cy)

    low[2] = jnp.minimum(low[1], hear(heard_ends, 1))
    relayed(3)
    tell(low.at[2], plane, heard_plane, 2)

    def corners():
        for face in (2, 3):
            for c in range(NF):
                row = (face * NF + c) * ROWS
                west, east = c * ROWS, (NF + c) * ROWS
                west0, east0 = c * 16, (NF + c) * 16
                for g in range(2):
                    side = g if face == 2 else 31 - g
                    for t, source in ((0, west), (1, west + 32), (30, east + 32), (31, east)):
                        far[pl.ds(row + 32 * g + t, 1), :] = far[pl.ds(source + side, 1), :]
                side = 1 if face == 2 else 14
                far[pl.ds(row + 64, 1), :] = far0[pl.ds(west0 + side, 1), :]
                far[pl.ds(row + 65, 1), :] = far[pl.ds(west + 64 + side, 1), :]
                far[pl.ds(row + 78, 1), :] = far[pl.ds(east + 64 + side, 1), :]
                far[pl.ds(row + 79, 1), :] = far0[pl.ds(east0 + side, 1), :]

    def fatten(face):
        for c in range(NF):
            row = (face * NF + c) * ROWS
            for g in range(2):
                far[pl.ds(row + 32 * g + 2, 28), :] = far_lean[pl.ds((face - 2) * 256 + (2 * c + g) * 28, 28), :]
            far[pl.ds(row + 66, 8), :] = far_lean[pl.ds((face - 2) * 256 + 224 + 8 * c, 8), :]
            far[pl.ds(row + 74, 4), :] = far_lean[pl.ds(512 + (face - 2) * 16 + 4 * c, 4), :]

    def shallow(face):
        for c in range(NF):
            row = (face * NF + c) * ROWS
            far0[pl.ds((face * NF + c) * 16, 16), :] = restricted(far, row, row + 32)

    ghosts = ghost_maker(own, own0, far, far0, relation_v, half_v, near_v, edge, coarse)

    def into(ref):
        def store(c, j, value):
            ref[c, j] = value

        return store

    def apply_x(c, i, change):
        cx[c, i] = cx[c, i] + change

    def join(n, carry):
        low_x, low_y = pl.multiple_of(n // 4 * 8, 8), pl.multiple_of(lax.rem(n, 4) * 8, 8)
        for c in range(NF):
            turned = jnp.swapaxes(cy[c, pl.ds(low_y, 8), pl.ds(low_x, 8), :], 0, 1)
            at = (c, pl.ds(low_x, 8), pl.ds(low_y, 8))
            cx[at] = cx[at] + turned
        return carry

    lax.fori_loop(0, 16, join, 0)

    arrived(0)
    shallow(0)
    ghosts(1, into(px))
    rim(lambda c, j: px[c, j], 1, 1, apply_x)
    def apply_y(c, j, change):
        rows = pl.ds(c * CELLS * CELLS + j, CELLS, stride=CELLS)
        cx2[rows, :] = cx2[rows, :] + change

    arrived(1)
    shallow(1)
    ghosts(0, into(px))
    rim(lambda c, j: px[c, j], 1, 0, apply_x)
    corners()
    fatten(2)
    shallow(2)
    ghosts(3, into(py))
    rim(lambda c, j: py[c, j], 2, 3, apply_y)

    lowest = jnp.minimum(low[2], hear(heard_plane, 2))
    time_step = COURANT * jnp.min(lowest, axis=1, keepdims=True)
    step_out[...] = jnp.broadcast_to(time_step, (1, LANES))
    ratio_out[...] = 0.5 * (time_step / spacing)
    ratio = jnp.broadcast_to(ratio_out[...], (CELLS, LANES))

    def settle(i, carry):
        for c in range(NF):
            out[c, i] = px[c, i + 2] - ratio * cx[c, i]
        return carry

    lax.fori_loop(0, CELLS, settle, 0, unroll=2)

    for stage, slots in enumerate((heard_z, heard_ends, heard_plane)):
        pltpu.make_async_copy(slots, slots, low_send.at[stage]).wait()

    for k in range(NSLOT):

        @pl.when(within(curve[k]))
        def _():
            block = rest_send.at[pl.ds(2 * k, 2)]
            pltpu.make_async_copy(block, block, rest_sem_send.at[k]).wait()

    arrived(2)
    fatten(3)
    shallow(3)
    for k in range(NSLOT):

        @pl.when(within(curve[k]))
        def _():
            block = send.at[pl.ds(k * SEND, SEND)]
            pltpu.make_async_copy(block, block, bulk_send.at[k]).wait()


def deliver(advanced, step, ratio, py, own, own0, far, far0, relation_v, half_v, near_v, out, step_out,
            one, south, turn, outer, edge, coarse, sem):
    copies = [
        pltpu.make_async_copy(advanced.at[c, :, pl.ds(8, 24)], out.at[c, :, pl.ds(8, 24)], sem.at[c])
        for c in range(NF)
    ]
    for copy in copies:
        copy.start()
    one[...] = step[:, pl.ds(0, 1)]
    copies.append(pltpu.make_async_copy(one, step_out, sem.at[2 * NF]))
    copies[-1].start()

    def store(c, j, value):
        outer[c, j] = value

    def load(c, j):
        return outer[c, j] if j < 2 else py[c, j]

    def keep(c, j, change):
        turn[c, j] = change

    ghost_maker(own, own0, far, far0, relation_v, half_v, near_v, edge, coarse)(2, store)
    rim(load, 2, 2, keep)
    for c in range(NF):
        turn[c, pl.ds(2, 6)] = jnp.zeros((6, CELLS, LANES), F32)
        for n in range(4):
            rows = pl.ds(8 * n, 8)
            south[c, rows] = advanced[c, rows, pl.ds(0, 8)] - ratio[...] * jnp.swapaxes(turn[c, :, rows, :], 0, 1)
        copies.append(pltpu.make_async_copy(south.at[c], out.at[c, :, pl.ds(0, 8)], sem.at[NF + c]))
        copies[-1].start()
    for copy in copies:
        copy.wait()


def on_device(fields, patch_level, relation, face_half, neighbour, send_list):
    any_space = pl.BlockSpec(memory_space=pl.ANY)
    vmem = pl.BlockSpec(memory_space=pltpu.VMEM)
    cube = (NF, CELLS, CELLS, LANES)
    held = (
        pltpu.VMEM(cube, F32),
        pltpu.VMEM((1, LANES), F32),
        pltpu.VMEM((1, LANES), F32),
        pltpu.VMEM((NF, PLANES, CELLS, LANES), F32),
        pltpu.VMEM((16 * ROWS, LANES), F32),
        pltpu.VMEM((256, LANES), F32),
        pltpu.VMEM((16 * ROWS, LANES), F32),
        pltpu.VMEM((256, LANES), F32),
        pltpu.VMEM((4, LANES), jnp.int32),
        pltpu.VMEM((4, LANES), jnp.int32),
        pltpu.VMEM((4, 2, LANES), jnp.int32),
    )
    results = pl.pallas_call(
        body,
        out_shape=held,
        in_specs=[any_space] * 6,
        out_specs=(vmem,) * len(held),
        scratch_shapes=[
            pltpu.VMEM((NF, PLANES, CELLS, LANES), F32),
            pltpu.VMEM(cube, F32),
            pltpu.VMEM(cube, F32),
            pltpu.VMEM((1, LANES), jnp.int32),
            pltpu.VMEM((SEND, NSLOT), jnp.int32),
            pltpu.VMEM((5 * LANES, LANES), F32),
            pltpu.VMEM((5 * LANES, LANES), F32),
            pltpu.VMEM((LANES, LANES), F32),
            pltpu.VMEM((LANES, TILES * LANES), F32),
            pltpu.VMEM((LANES, TILES * LANES), F32),
            pltpu.VMEM((REST, LANES), F32),
            pltpu.VMEM((REST, LANES), F32),
            pltpu.VMEM((48, LANES), F32),
            pltpu.VMEM((CELLS, LANES), F32),
            pltpu.VMEM((3, 1, LANES), F32),
            pltpu.VMEM((2 * NEAR_Z, 1, LANES), F32),
            pltpu.VMEM((2, 1, LANES), F32),
            pltpu.VMEM((2 * DIM_X * DIM_Y - 1, 1, LANES), F32),
            pltpu.SemaphoreType.DMA((2 * NF,)),
            pltpu.SemaphoreType.DMA((NF,)),
            pltpu.SemaphoreType.DMA((5,)),
            pltpu.SemaphoreType.DMA((NSLOT,)),
            pltpu.SemaphoreType.DMA((len(PARTS), NSLOT)),
            pltpu.SemaphoreType.DMA((NSLOT,)),
            pltpu.SemaphoreType.DMA((NSLOT,)),
            pltpu.SemaphoreType.DMA((3,)),
            pltpu.SemaphoreType.DMA((3,)),
            pltpu.SemaphoreType.REGULAR((4,)),
        ],
        compiler_params=pltpu.CompilerParams(
            collective_id=0, has_side_effects=True, vmem_limit_bytes=48 << 20
        ),
    )(*(
        pltpu.with_memory_space_constraint(operand, pltpu.HBM)
        for operand in (
            fields,
            patch_level.reshape(1, LANES),
            relation.T,
            face_half.T,
            jnp.transpose(neighbour, (1, 2, 0)),
            send_list[0].T,
        )
    ))
    advanced, step = pl.pallas_call(
        deliver,
        out_shape=(jax.ShapeDtypeStruct(cube, F32), jax.ShapeDtypeStruct((1, 1), F32)),
        in_specs=[vmem] * len(held),
        out_specs=(any_space, any_space),
        scratch_shapes=[
            pltpu.VMEM((1, 1), F32),
            pltpu.VMEM((NF, CELLS, 8, LANES), F32),
            pltpu.VMEM((NF, 8, CELLS, LANES), F32),
            pltpu.VMEM((NF, 2, CELLS, LANES), F32),
            pltpu.VMEM((48, LANES), F32),
            pltpu.VMEM((CELLS, LANES), F32),
            pltpu.SemaphoreType.DMA((2 * NF + 1,)),
        ],
        compiler_params=pltpu.CompilerParams(vmem_limit_bytes=48 << 20),
    )(*(pltpu.with_memory_space_constraint(result, pltpu.VMEM) for result in results))
    return advanced, step.reshape(())


def solution(mesh):
    return jax.shard_map(
        on_device,
        mesh=mesh,
        in_specs=(
            P(None, None, None, "patch"),
            P("patch"),
            P("patch", None),
            P("patch", None),
            P("patch", None, None),
            P("patch", None, None),
        ),
        out_specs=(P(None, None, None, "patch"), P()),
        check_vma=False,
    )
```

time: 35.6 us -> 35.4 us (level)
  no operation moved by 1% of the time
where the time goes in v6:
time: 35.4 us; the launch traced here: 35.1 us
  Pallas kernels  34.4 us (97%)
  between operations  0.64 us (2%)
    pallas_call x1, Pallas kernels, on_device(): pl.pallas_call(body, out_shape=held, in_specs=[any_space] * 6, out_specs=...  32.9 us
    pallas_call x1, Pallas kernels, on_device(): pl.pallas_call(deliver, out_shape=(jax.ShapeDtypeStruct(cube, F32), jax.S...  1.58 us

profile of v6, /device:TPU:1, one launch (start us, length us, event | category | flops | bytes accessed | tf_op | source)
XLA Modules:
  0.0 35.1 jit_solution(2784364823597870451)
XLA Ops:
  0.6 32.9 %shard_map.77 = (f32[4,32,32,128]{3,2,1,0:T(8,128)S(1)}, f32[1,128]{1,0:T(1,128)S(1)}, f32[1,128]{1,0:T(1,128)S(1)}, f32[4,36,32,128]{3,2,1,0:T(8,128)S(1)}, f32...) custom-call(f32[4,32,32,128]{3,2,1,0:T(8,128)} %fields.1, ...), custom_call_target="tpu_custom_call" | custom-call | tf_op jit(solution)/shard_map/pallas_call | solution.py:534
  33.5 1.6 %shard_map.78 = (f32[4,32,32,128]{3,2,1,0:T(8,128)}, f32[1,1]{1,0:T(1,128)}) custom-call(f32[4,32,32,128]{3,2,1,0:T(8,128)S(1)} %get-tuple-element.15.advanced, f32[1,128]{1,0:T(1,128)S(1)} %get-tuple-element.16.step, f32[1,128]{1,0:T(1,128)S(1)} %get-tuple-element.17.ratio, f32[4,36,32,128]{3,2,1,0:T(8,128)S(1)} %get-tuple-element.18.py, ...), custom_call_target="tpu_custom_call" | custom-call | tf_op jit(solution)/shard_map/pallas_call | solution.py:583
